TPU v7x, 32 devices: a whole 2x2x4 slice. The times are simulated.
32 devices in a mesh: cuts: 2 (over y), qa: 16 (over z, x, core).
Axes of the slice: x: 2, y: 2, z: 4, core: 2. Of those that a mesh axis runs over, the one named last changes fastest.
Arguments:
- state: float32 [2, 4194304], P(None, ('cuts', 'qa')), parts along dimension 1, may hold values from -6 to 6
- unitaries: float32 [12, 2, 128, 128], replicated, may hold values from -1 to 1, as said below
- gate_order: int32 [12], replicated, may hold values from 0 to 11, each once
- gate_starts: int32 [12], replicated, may hold values from 0 to 1
- pair_gates: float32 [2, 2, 2, 2], replicated, may hold values from -1 to 1, as said below
Outputs:
- final_state: float32 [2, 4194304], P(None, ('cuts', 'qa')), parts along dimension 1
There are 2 independent parts, one for each index of `cuts`. A program takes and returns all parts, laid end to end along the dimension named above; an argument that names none is the same for every part. Nothing has to cross between parts.
Inputs may be any that keep to these rules, and one draw needn't show every extreme that they name: For every k, unitaries[k, 0] + i unitaries[k, 1] is a unitary matrix. For each p, pair_gates[p, 0] + i pair_gates[p, 1] is a unitary 2 x 2 matrix. `gate_order`: A permutation of 0 .. 11.
All inputs are finite; a program needn't handle non-finite values.
Results may differ from a plain program's by a relative error of at most 0.0003.
Values sent between devices are 32-bit elements; how exact they have to be, the bound alone decides.
No kernel may reach another device: no remote copies, remote signals or barrier semaphores. Data moves between devices by JAX's collectives and lax.ppermute only.
A program may use at most 64 MiB of HBM per device.

v0:
```python
from functools import partial

import jax
import jax.numpy as jnp
from jax import lax
from jax.experimental import pallas as pl
from jax.experimental.pallas import tpu as pltpu
from jax.sharding import PartitionSpec as P


HIGH = lax.Precision.HIGHEST
F32 = jnp.float32
BF16 = jnp.bfloat16


def mix(mat, vec):
    return jnp.einsum("ij,ajb->aib", mat, vec, precision=HIGH)


def dense_branch(re_part, im_part, u_re, u_im, offset):
    gdim = u_re.shape[0]
    gq = gdim.bit_length() - 1
    block = 2 ** (gq + offset)
    shaped_re = re_part.reshape(-1, gdim, block)
    shaped_im = im_part.reshape(-1, gdim, block)
    new_re = mix(u_re, shaped_re) - mix(u_im, shaped_im)
    new_im = mix(u_re, shaped_im) + mix(u_im, shaped_re)
    return (new_re.reshape(-1), new_im.reshape(-1))


def dense_gate(stacked, unitaries, gate_order, gate_starts, k):
    chosen = unitaries[gate_order[k]]
    branches = [partial(dense_branch, offset=0), partial(dense_branch, offset=1)]
    new_re, new_im = lax.switch(
        gate_starts[k], branches, stacked[0], stacked[1], chosen[0], chosen[1]
    )
    return jnp.stack([new_re, new_im])


def one_qubit(stacked, gate, qubit):
    shaped = stacked.reshape(2, -1, 2, 2**qubit)
    u_re, u_im = (gate[0], gate[1])
    new_re = jnp.einsum("bc,acx->abx", u_re, shaped[0], precision=HIGH) - jnp.einsum(
        "bc,acx->abx", u_im, shaped[1], precision=HIGH
    )
    new_im = jnp.einsum("bc,acx->abx", u_re, shaped[1], precision=HIGH) + jnp.einsum(
        "bc,acx->abx", u_im, shaped[0], precision=HIGH
    )
    return jnp.stack([new_re, new_im]).reshape(2, -1)


def swap_qubits(stacked):
    devices = lax.axis_size("qa")
    shaped = stacked.reshape(2, devices, -1)
    moved = lax.all_to_all(shaped, "qa", split_axis=1, concat_axis=1, tiled=True)
    return moved.reshape(2, -1)


def general(state, unitaries, gate_order, gate_starts, pair_gates):
    local_bits = state.shape[1].bit_length() - 1
    global_bits = lax.axis_size("qa").bit_length() - 1
    ngates = unitaries.shape[0]
    third = ngates // 3
    stacked = state
    for k in range(third):
        stacked = dense_gate(stacked, unitaries, gate_order, gate_starts, k)
    stacked = one_qubit(stacked, pair_gates[0], local_bits - 1)
    stacked = swap_qubits(stacked)
    for k in range(third, 2 * third):
        stacked = dense_gate(stacked, unitaries, gate_order, gate_starts, k)
    stacked = one_qubit(stacked, pair_gates[1], local_bits - global_bits)
    stacked = swap_qubits(stacked)
    for k in range(2 * third, ngates):
        stacked = dense_gate(stacked, unitaries, gate_order, gate_starts, k)
    return stacked


def split(x):
    hi = x.astype(BF16)
    return hi, (x - hi.astype(F32)).astype(BF16)


def dot3(w_hi, w_lo, x):
    x_hi, x_lo = split(x)
    return jnp.dot(
        jnp.concatenate([w_hi, w_hi, w_lo], axis=1),
        jnp.concatenate([x_hi, x_lo, x_hi], axis=0),
        preferred_element_type=F32,
    )


def embed(re, im):
    return jnp.concatenate(
        [jnp.concatenate([re, -im], axis=1), jnp.concatenate([im, re], axis=1)], axis=0
    )


def my_bits():
    me = lax.axis_index("qa")
    return lax.rem(me, 2), lax.rem(lax.div(me, 2), 2)


def compose(first, count, flip, order, starts, unit, m_re, m_im):
    gdim = unit.shape[-1]
    row = lax.broadcasted_iota(jnp.int32, (2 * gdim, 2 * gdim), 0)
    col = lax.broadcasted_iota(jnp.int32, (2 * gdim, 2 * gdim), 1)
    one = jnp.where(row == jnp.bitwise_xor(col, flip), 1.0, 0.0).astype(F32)
    for j in range(2):
        m_re[j] = one[:, j * gdim : (j + 1) * gdim]
    m_im[...] = jnp.zeros_like(m_im)

    def step(k, carry):
        gate = order[k]
        w_hi, w_lo = split(embed(unit[gate, 0], unit[gate, 1]))

        def run(rows):
            blocks = [(j, r) for r in rows for j in range(2)]
            x = jnp.concatenate(
                [jnp.concatenate([m_re[j, r, :], m_im[j, r, :]], axis=0) for j, r in blocks],
                axis=1,
            )
            y = dot3(w_hi, w_lo, x)
            for i, (j, r) in enumerate(blocks):
                m_re[j, r, :] = y[:gdim, gdim * i : gdim * (i + 1)]
                m_im[j, r, :] = y[gdim:, gdim * i : gdim * (i + 1)]

        @pl.when(starts[k] == 0)
        def _():
            run([pl.ds(b * gdim, gdim) for b in range(2)])

        @pl.when(starts[k] != 0)
        def _():
            run([pl.ds(b, gdim, stride=2) for b in range(2)])

        return carry

    lax.fori_loop(first, first + count, step, 0)


def put(ref, re, im):
    ref[0], ref[1] = split(embed(re, im))


def whole(m):
    return jnp.concatenate([m[j] for j in range(2)], axis=1)


def parts_of(ref, at, rows):
    return jnp.concatenate(
        [ref[at, pl.ds(0, rows, stride=2), :], ref[at, pl.ds(1, rows, stride=2), :]], axis=0
    )


def front_kernel(count, order, starts, unit, state, w_ref, kept0, kept1, m_re, m_im, u, s, sems):
    _, h1 = my_bits()
    copies = [
        pltpu.make_async_copy(unit, u, sems.at[0]),
        pltpu.make_async_copy(state.at[pl.ds(h1 * 2, 2)], s, sems.at[1]),
    ]
    for c in copies:
        c.start()
    copies[0].wait()
    compose(0, count, 0, order, starts, u, m_re, m_im)
    put(w_ref, whole(m_re), whole(m_im))
    copies[1].wait()
    rows = s.shape[1] // 2
    x = jnp.concatenate([parts_of(s, c, rows) for c in range(2)], axis=1)
    y = dot3(w_ref[0], w_ref[1], x)
    lanes = s.shape[2]
    kept0[0] = y[:, :lanes]
    kept1[0] = y[:, lanes:]


def second_kernel(count, order, starts, pair, unit, w_ref, m_re, m_im):
    gdim = unit.shape[-1]
    half = gdim // 2
    h0, h1 = my_bits()
    compose(count, count, h1 * gdim + h0 * half, order, starts, unit, m_re, m_im)
    re, im = [], []
    for k in range(2):
        at = lax.rem(h1 + k, 2) * gdim
        r, i = 0.0, 0.0
        for b in range(2):
            rows = pl.ds(pl.multiple_of(at + b * half, half), half)
            v_re, v_im = pair[1, 0, h0, b], pair[1, 1, h0, b]
            x_re, x_im = (
                jnp.concatenate([m[j, rows, :] for j in range(2)], axis=1) for m in (m_re, m_im)
            )
            r += v_re * x_re - v_im * x_im
            i += v_re * x_im + v_im * x_re
        re.append(r)
        im.append(i)
    put(w_ref, jnp.concatenate(re, axis=0), jnp.concatenate(im, axis=0))


def third_kernel(count, order, starts, unit, w_ref, m_re, m_im):
    compose(2 * count, count, 0, order, starts, unit, m_re, m_im)
    put(w_ref, whole(m_re), whole(m_im))


def first_kernel(w_ref, raw, out):
    rows = raw.shape[1] // 2
    out[0] = dot3(w_ref[0], w_ref[1], parts_of(raw, 0, rows))


def middle_kernel(w1_ref, w2_ref, own_kept, other_kept, own_came, other_came, keep, back):
    lanes = own_kept.shape[2]
    dim = own_kept.shape[1] // 2
    part = dim // 4
    sources = (own_kept, other_kept, own_came, other_came)
    cols = []
    for f in range(4):
        cols.append(
            jnp.concatenate(
                [s[0, pl.ds(p * dim + f * part, part), :] for p in range(2) for s in sources],
                axis=0,
            )
        )
    y = dot3(w1_ref[0], w1_ref[1], jnp.concatenate(cols, axis=1))
    cols = []
    for k in range(2):
        cols.append(
            jnp.concatenate(
                [
                    y[(2 * p + k) * part : (2 * p + k + 1) * part, f * lanes : (f + 1) * lanes]
                    for p in range(2)
                    for f in range(4)
                ],
                axis=0,
            )
        )
    z = dot3(w2_ref[0], w2_ref[1], jnp.concatenate(cols, axis=1))
    keep[0] = z[:, :lanes]
    back[0] = z[:, lanes:]


def last_kernel(pair, keep, back, *refs):
    out = refs[-1]
    _, h1 = my_bits()
    b = pl.program_id(0)
    rows = keep.shape[1] // 2
    k_re, k_im = keep[0, :rows, :], keep[0, rows:, :]
    b_re, b_im = back[0, :rows, :], back[0, rows:, :]
    v_re, v_im = pair[0, 0, b, h1], pair[0, 1, b, h1]
    u_re, u_im = pair[0, 0, b, 1 - h1], pair[0, 1, b, 1 - h1]
    out[0, 0, pl.ds(0, rows, stride=2), :] = v_re * k_re - v_im * k_im + u_re * b_re - u_im * b_im
    out[0, 0, pl.ds(1, rows, stride=2), :] = v_re * k_im + v_im * k_re + u_re * b_im + u_im * b_re


VM = pl.BlockSpec(memory_space=pltpu.VMEM)
SM = pl.BlockSpec(memory_space=pltpu.SMEM)
HB = pl.BlockSpec(memory_space=pltpu.HBM)


def cost(outs, args, flops):
    nbytes = sum(a.size * a.dtype.itemsize for a in (*outs, *args))
    return pl.CostEstimate(flops=flops, bytes_accessed=nbytes, transcendentals=0)


PARAMS = pltpu.CompilerParams(vmem_limit_bytes=16 * 2**20)


def call(body, outs, args, specs, scratch=(), flops=0):
    return pl.pallas_call(
        body,
        out_shape=outs,
        in_specs=specs,
        out_specs=[VM] * len(outs),
        scratch_shapes=scratch,
        cost_estimate=cost(outs, args, flops),
        compiler_params=PARAMS,
    )(*args)


def finish(pair, keep, back, shape, chunk, before=None):
    args = [pair, keep, back] + ([] if before is None else [before])
    return pl.pallas_call(
        last_kernel,
        out_shape=shape,
        grid=(2,),
        in_specs=[SM, VM, VM] + ([] if before is None else [HB]),
        out_specs=pl.BlockSpec((1, 1, *shape.shape[2:]), lambda i: (i, chunk, 0, 0)),
        input_output_aliases={} if before is None else {3: 0},
        cost_estimate=cost([shape], [keep, back], 0),
        compiler_params=PARAMS,
    )(*args)


def paired(state, unitaries, gate_order, gate_starts, pair):
    devices = lax.axis_size("qa")
    count = unitaries.shape[0] // 3
    gdim = unitaries.shape[-1]
    lanes, rows, dim = gdim, 4 * gdim, 2 * gdim
    f32 = partial(jax.ShapeDtypeStruct, dtype=F32)
    bf16 = partial(jax.ShapeDtypeStruct, dtype=BF16)
    tie = lax.optimization_barrier
    far = partial(pltpu.with_memory_space_constraint, memory_space=pltpu.HBM)
    _, h1 = my_bits()

    def other(v, bit):
        return lax.ppermute(v, "qa", [(i, i ^ bit) for i in range(devices)])

    def block_of(v, c):
        return lax.dynamic_slice_in_dim(v, (1 - h1) * 2 + c, 1, axis=0)

    view = state.reshape(2, -1, lanes).transpose(1, 0, 2).reshape(4, rows, lanes)
    came = [other(block_of(view, c), 2) for c in range(2)]
    scratch = [pltpu.VMEM((2, dim, gdim), F32)] * 2
    step = 3 * 2 * (2 * gdim) * (2 * gdim) * (4 * gdim)
    block = f32((1, rows, lanes))
    w0, *kept = call(
        partial(front_kernel, count),
        [bf16((2, rows, rows)), block, block],
        [far(gate_order), far(gate_starts), far(unitaries), far(view)],
        [SM, SM, HB, HB],
        scratch
        + [
            pltpu.VMEM(unitaries.shape, F32),
            pltpu.VMEM((2, rows, lanes), F32),
            pltpu.SemaphoreType.DMA((2,)),
        ],
        flops=count * step + 6 * rows * rows * 2 * lanes,
    )
    kept_other = [other(k, 1) for k in kept]
    (w1,) = call(
        partial(second_kernel, count),
        [bf16((2, dim, rows))],
        [gate_order, gate_starts, pair, unitaries],
        [SM, SM, SM, VM],
        scratch,
        flops=count * step,
    )

    def enter(v):
        flops = 6 * rows * rows * lanes
        return call(first_kernel, [block], [w0, v], [VM, VM], flops=flops)[0]

    def middle(c, mine):
        return call(
            middle_kernel,
            [block, block],
            [w1, w2, kept[c], kept_other[c], mine, other(mine, 1)],
            [VM] * 6,
            flops=6 * rows * rows * 4 * lanes,
        )

    came[0], w1 = tie((came[0], w1))
    mine = enter(came[0])
    order_then, mine = tie((gate_order, mine))
    (w2,) = call(
        partial(third_kernel, count),
        [bf16((2, rows, rows))],
        [order_then, gate_starts, unitaries],
        [SM, SM, VM],
        scratch,
        flops=count * step,
    )
    keep0, back0 = middle(0, mine)
    came[1], back0 = tie((came[1], back0))
    back0 = other(back0, 2)
    keep1, back1 = middle(1, enter(came[1]))
    back0, keep1 = tie((back0, keep1))
    back1 = other(back1, 2)
    whole_shape = f32((2, 2, rows, lanes))
    out = finish(pair, keep0, back0, whole_shape, 0)
    out = finish(pair, keep1, back1, whole_shape, 1, out)
    return out.reshape(-1, 2, lanes).transpose(1, 0, 2).reshape(2, -1)


def meets_two(state, unitaries, devices):
    local_bits = state.shape[1].bit_length() - 1
    global_bits = devices.bit_length() - 1
    top = 2 * (unitaries.shape[-1].bit_length() - 1) + 1
    met = top - (local_bits - global_bits)
    return met == 2 and local_bits == top + 2 and global_bits >= 2


def shards(*args):
    if meets_two(args[0], args[1], lax.axis_size("qa")):
        return paired(*args)
    return general(*args)


def solution(mesh):
    placed = (P(None, ("cuts", "qa")), P(), P(), P(), P())
    return jax.shard_map(
        shards, mesh=mesh, in_specs=placed, out_specs=P(None, ("cuts", "qa")), check_vma=False
    )
```

profile of v0, /device:TPU:0, one launch (start us, length us, event | category | flops | bytes accessed | tf_op | source)
XLA Modules:
  0.0 37.1 jit_solution(15317821405423218518)
XLA Ops:
  0.0 1.1 %constant_dynamic-slice_fusion = (f32[1,512,128]{2,1,0:T(8,128)S(1)}, f32[1,512,128]{2,1,0:T(8,128)S(1)}) fusion(f32[4,512,128]{2,1,0:T(8,128)} %bitcast.10, s32[]{:T(128)S(6)} %select_n.7, s32[]{:T(128)S(6)} %select_n.6), kind=kLoop, calls=%fused_computation | loop fusion | bytes 1048584 | tf_op jit(solution)/shard_map/dynamic_slice | solution.py:304
  1.1 0.0 copy-start
  1.1 0.0 copy-start.1
  1.1 0.0 copy-start.2
  1.1 0.0 copy-start.3
  1.1 3.0 %collective-permute-start.1 = (f32[1,512,128]{2,1,0:T(8,128)S(1)}, f32[1,512,128]{2,1,0:T(8,128)S(1)}, u32[]{:S(2)}, u32[]{:S(2)}) collective-permute-start(f32[1,512,128]{2,1,0:T(8,128)S(1)} %get-tuple-element.35), channel_id=1, source_target_pairs={{0,2},{1,3},{2,0},{3,1},{4,6},{5,7},{6,4},{7,5},{8,10},{9,11},{10,... | collective-permute-start | bytes 786440 | tf_op jit(solution)/shard_map/ppermute | solution.py:301
  4.1 4.5 %shard_map.56 = (bf16[2,512,512]{2,1,0:T(8,128)(2,1)S(1)}, f32[1,512,128]{2,1,0:T(8,128)S(1)}, f32[1,512,128]{2,1,0:T(8,128)S(1)}) custom-call(s32[12]{0:T(128)} %order.4, s32[12]{0:T(128)} %starts.5, f32[12,2,128,128]{3,2,1,0:T(8,128)} %unit.5, f32[4,512,128]{2,1,0:T(8,128)} %bitcast.11), custom_call_target="tpu_custom_call" | custom-call | flops 1207959552 | bytes 4194400 | tf_op jit(solution)/shard_map/pallas_call | solution.py:264
  8.7 0.1 collective-permute-start.2
  8.8 0.0 copy-done
  8.8 0.0 copy-done.1
  8.8 0.0 copy-done.2
  8.8 0.0 copy-done.3
  8.8 2.4 %shard_map.55.w1_ref = bf16[2,256,512]{2,1,0:T(8,128)(2,1)S(1)} custom-call(s32[12]{0:T(128)S(1)} %copy-done.2, s32[12]{0:T(128)S(1)} %copy-done.3, f32[2,2,2,2]{3,2,1,0:T(2,128)S(1)} %copy-done, f32[12,2,128,128]{3,2,1,0:T(8,128)S(1)} %copy-done.1), custom_call_target="tpu_custom_call" | custom-call | flops 805306368 | bytes 2097312 | tf_op jit(solution)/shard_map/pallas_call | solution.py:264
  11.2 0.0 collective-permute-done.1.raw
  11.2 0.6 %shard_map.57.own_came = f32[1,512,128]{2,1,0:T(8,128)S(1)} custom-call(bf16[2,512,512]{2,1,0:T(8,128)(2,1)S(1)} %get-tuple-element.21.w_ref, f32[1,512,128]{2,1,0:T(8,128)S(1)} %collective-permute-done.1.raw), custom_call_target="tpu_custom_call" | custom-call | flops 201326592 | bytes 1572864 | tf_op jit(solution)/shard_map/pallas_call | solution.py:264
  11.8 0.5 %collective-permute-start.3 = (f32[1,512,128]{2,1,0:T(8,128)S(1)}, f32[1,512,128]{2,1,0:T(8,128)S(1)}, u32[]{:S(2)}, u32[]{:S(2)}) collective-permute-start(f32[1,512,128]{2,1,0:T(8,128)S(1)} %shard_map.57.own_came), channel_id=1, source_target_pairs={{0,1},{1,0},{2,3},{3,2},{4,5},{5,4},{6,7},{7,6},{8,9},{9,8},{10,11... | collective-permute-start | bytes 786440 | tf_op jit(solution)/shard_map/ppermute | solution.py:301
  12.4 0.6 %collective-permute-start = (f32[1,512,128]{2,1,0:T(8,128)S(1)}, f32[1,512,128]{2,1,0:T(8,128)S(1)}, u32[]{:S(2)}, u32[]{:S(2)}) collective-permute-start(f32[1,512,128]{2,1,0:T(8,128)S(1)} %get-tuple-element.36), channel_id=1, source_target_pairs={{0,2},{1,3},{2,0},{3,1},{4,6},{5,7},{6,4},{7,5},{8,10},{9,11},{10,... | collective-permute-start | bytes 786440 | tf_op jit(solution)/shard_map/ppermute | solution.py:301
  12.9 0.2 collective-permute-start.5
  13.1 2.4 %shard_map.58.w2_ref = bf16[2,512,512]{2,1,0:T(8,128)(2,1)S(1)} custom-call(s32[12]{0:T(128)S(1)} %copy-done.2, s32[12]{0:T(128)S(1)} %copy-done.3, f32[12,2,128,128]{3,2,1,0:T(8,128)S(1)} %copy-done.1), custom_call_target="tpu_custom_call" | custom-call | flops 805306368 | bytes 2621536 | tf_op jit(solution)/shard_map/pallas_call | solution.py:264
  15.5 0.0 collective-permute-done.2.other_kept
  15.5 0.0 collective-permute-done.3.other_came
  15.5 1.2 %shard_map.59 = (f32[1,512,128]{2,1,0:T(8,128)S(1)}, f32[1,512,128]{2,1,0:T(8,128)S(1)}) custom-call(bf16[2,256,512]{2,1,0:T(8,128)(2,1)S(1)} %shard_map.55.w1_ref, bf16[2,512,512]{2,1,0:T(8,128)(2,1)S(1)} %shard_map.58.w2_ref, f32[1,512,128]{2,1,0:T(8,128)S(1)} %get-tuple-element.24.own_kept, f32[1,512,128]{2,1,0:T(8,128)S(1)} %collective-permute-done.2.other_kept, ...), custom_call_target="tpu_custom_call" | custom-call | flops 805306368 | bytes 3145728 | tf_op jit(solution)/shard_map/pallas_call | solution.py:264
  16.7 4.0 %collective-permute-done.raw = f32[1,512,128]{2,1,0:T(8,128)S(1)} collective-permute-done((f32[1,512,128]{2,1,0:T(8,128)S(1)}, f32[1,512,128]{2,1,0:T(8,128)S(1)}, u32[]{:S(2)}, u32[]{:S(2)}) %collective-permute-start) | collective-permute-done | bytes 262176 | tf_op jit(solution)/shard_map/ppermute | solution.py:301
  20.6 0.6 %shard_map.60.own_came = f32[1,512,128]{2,1,0:T(8,128)S(1)} custom-call(bf16[2,512,512]{2,1,0:T(8,128)(2,1)S(1)} %get-tuple-element.21.w_ref, f32[1,512,128]{2,1,0:T(8,128)S(1)} %collective-permute-done.raw), custom_call_target="tpu_custom_call" | custom-call | flops 201326592 | bytes 1572864 | tf_op jit(solution)/shard_map/pallas_call | solution.py:264
  21.2 0.1 collective-permute-start.6
  21.3 1.0 %collective-permute-start.4 = (f32[1,512,128]{2,1,0:T(8,128)S(1)}, f32[1,512,128]{2,1,0:T(8,128)S(1)}, u32[]{:S(2)}, u32[]{:S(2)}) collective-permute-start(f32[1,512,128]{2,1,0:T(8,128)S(1)} %get-tuple-element.27), channel_id=1, source_target_pairs={{0,2},{1,3},{2,0},{3,1},{4,6},{5,7},{6,4},{7,5},{8,10},{9,11},{10,... | collective-permute-start | bytes 786440 | tf_op jit(solution)/shard_map/ppermute | solution.py:301
  22.3 0.0 collective-permute-done.5.other_kept
  22.3 0.5 %collective-permute-done.6.other_came = f32[1,512,128]{2,1,0:T(8,128)S(1)} collective-permute-done((f32[1,512,128]{2,1,0:T(8,128)S(1)}, f32[1,512,128]{2,1,0:T(8,128)S(1)}, u32[]{:S(2)}, u32[]{:S(2)}) %collective-permute-start.6) | collective-permute-done | bytes 262176 | tf_op jit(solution)/shard_map/ppermute | solution.py:301
  22.8 1.2 %shard_map.61 = (f32[1,512,128]{2,1,0:T(8,128)S(1)}, f32[1,512,128]{2,1,0:T(8,128)S(1)}) custom-call(bf16[2,256,512]{2,1,0:T(8,128)(2,1)S(1)} %shard_map.55.w1_ref, bf16[2,512,512]{2,1,0:T(8,128)(2,1)S(1)} %shard_map.58.w2_ref, f32[1,512,128]{2,1,0:T(8,128)S(1)} %get-tuple-element.28.own_kept, f32[1,512,128]{2,1,0:T(8,128)S(1)} %collective-permute-done.5.other_kept, ...), custom_call_target="tpu_custom_call" | custom-call | flops 805306368 | bytes 3145728 | tf_op jit(solution)/shard_map/pallas_call | solution.py:264
  24.0 1.0 %collective-permute-start.7 = (f32[1,512,128]{2,1,0:T(8,128)S(1)}, f32[1,512,128]{2,1,0:T(8,128)S(1)}, u32[]{:S(2)}, u32[]{:S(2)}) collective-permute-start(f32[1,512,128]{2,1,0:T(8,128)S(1)} %get-tuple-element.32), channel_id=1, source_target_pairs={{0,2},{1,3},{2,0},{3,1},{4,6},{5,7},{6,4},{7,5},{8,10},{9,11},{10,... | collective-permute-start | bytes 786440 | tf_op jit(solution)/shard_map/ppermute | solution.py:301
  25.0 5.6 %collective-permute-done.4.back = f32[1,512,128]{2,1,0:T(8,128)S(1)} collective-permute-done((f32[1,512,128]{2,1,0:T(8,128)S(1)}, f32[1,512,128]{2,1,0:T(8,128)S(1)}, u32[]{:S(2)}, u32[]{:S(2)}) %collective-permute-start.4) | collective-permute-done | bytes 262176 | tf_op jit(solution)/shard_map/ppermute | solution.py:301
  30.6 1.5 %shard_map.62.refs_0_ = f32[2,2,512,128]{3,2,1,0:T(8,128)} custom-call(f32[2,2,2,2]{3,2,1,0:T(2,128)S(1)} %copy-done, f32[1,512,128]{2,1,0:T(8,128)S(1)} %get-tuple-element.33.keep, f32[1,512,128]{2,1,0:T(8,128)S(1)} %collective-permute-done.4.back), custom_call_target="tpu_custom_call" | custom-call | bytes 1572864 | tf_op jit(solution)/shard_map/pallas_call | solution.py:277
  32.1 3.6 %collective-permute-done.7.back = f32[1,512,128]{2,1,0:T(8,128)S(1)} collective-permute-done((f32[1,512,128]{2,1,0:T(8,128)S(1)}, f32[1,512,128]{2,1,0:T(8,128)S(1)}, u32[]{:S(2)}, u32[]{:S(2)}) %collective-permute-start.7) | collective-permute-done | bytes 262176 | tf_op jit(solution)/shard_map/ppermute | solution.py:301
  35.6 1.5 %shard_map.63 = f32[2,2,512,128]{3,2,1,0:T(8,128)} custom-call(f32[2,2,2,2]{3,2,1,0:T(2,128)S(1)} %copy-done, f32[1,512,128]{2,1,0:T(8,128)S(1)} %get-tuple-element.31.keep, f32[1,512,128]{2,1,0:T(8,128)S(1)} %collective-permute-done.7.back, f32[2,2,512,128]{3,2,1,0:T(8,128)} %shard_map.62.refs_0_), custom_call_target="tpu_custom_call", output_to_operand_aliasing={{}: (3, {})} | custom-call | bytes 1572864 | tf_op jit(solution)/shard_map/pallas_call | solution.py:277
Async XLA Ops:
  1.1 7.7 %copy-start = (f32[2,2,2,2]{3,2,1,0:T(2,128)S(1)}, f32[2,2,2,2]{3,2,1,0:T(2,128)}, u32[]{:S(2)}) copy-start(f32[2,2,2,2]{3,2,1,0:T(2,128)} %pair.5) | copy-start | bytes 196
  1.1 7.7 %copy-start.1 = (f32[12,2,128,128]{3,2,1,0:T(8,128)S(1)}, f32[12,2,128,128]{3,2,1,0:T(8,128)}, u32[]{:S(2)}) copy-start(f32[12,2,128,128]{3,2,1,0:T(8,128)} %unit.5) | copy-start | bytes 4718596
  1.1 7.7 %copy-start.2 = (s32[12]{0:T(128)S(1)}, s32[12]{0:T(128)}, u32[]{:S(2)}) copy-start(s32[12]{0:T(128)} %order.4) | copy-start | bytes 148
  1.1 7.7 %copy-start.3 = (s32[12]{0:T(128)S(1)}, s32[12]{0:T(128)}, u32[]{:S(2)}) copy-start(s32[12]{0:T(128)} %starts.5) | copy-start | bytes 148
  1.1 10.1 %collective-permute-start.1 = (f32[1,512,128]{2,1,0:T(8,128)S(1)}, f32[1,512,128]{2,1,0:T(8,128)S(1)}, u32[]{:S(2)}, u32[]{:S(2)}) collective-permute-start(f32[1,512,128]{2,1,0:T(8,128)S(1)} %get-tuple-element.35), channel_id=1, source_target_pairs={{0,2},{1,3},{2,0},{3,1},{4,6},{5,7},{6,4},{7,5},{8,10},{9,11},{10,... | collective-permute-start | bytes 786440 | tf_op jit(solution)/shard_map/ppermute | solution.py:301
  8.7 6.8 %collective-permute-start.2 = (f32[1,512,128]{2,1,0:T(8,128)S(1)}, f32[1,512,128]{2,1,0:T(8,128)S(1)}, u32[]{:S(2)}, u32[]{:S(2)}) collective-permute-start(f32[1,512,128]{2,1,0:T(8,128)S(1)} %get-tuple-element.24.own_kept), channel_id=1, source_target_pairs={{0,1},{1,0},{2,3},{3,2},{4,5},{5,4},{6,7},{7,6},{8,9},{9,8},{10,11... | collective-permute-start | bytes 786440 | tf_op jit(solution)/shard_map/ppermute | solution.py:301
  11.8 3.7 %collective-permute-start.3 = (f32[1,512,128]{2,1,0:T(8,128)S(1)}, f32[1,512,128]{2,1,0:T(8,128)S(1)}, u32[]{:S(2)}, u32[]{:S(2)}) collective-permute-start(f32[1,512,128]{2,1,0:T(8,128)S(1)} %shard_map.57.own_came), channel_id=1, source_target_pairs={{0,1},{1,0},{2,3},{3,2},{4,5},{5,4},{6,7},{7,6},{8,9},{9,8},{10,11... | collective-permute-start | bytes 786440 | tf_op jit(solution)/shard_map/ppermute | solution.py:301
  12.4 8.3 %collective-permute-start = (f32[1,512,128]{2,1,0:T(8,128)S(1)}, f32[1,512,128]{2,1,0:T(8,128)S(1)}, u32[]{:S(2)}, u32[]{:S(2)}) collective-permute-start(f32[1,512,128]{2,1,0:T(8,128)S(1)} %get-tuple-element.36), channel_id=1, source_target_pairs={{0,2},{1,3},{2,0},{3,1},{4,6},{5,7},{6,4},{7,5},{8,10},{9,11},{10,... | collective-permute-start | bytes 786440 | tf_op jit(solution)/shard_map/ppermute | solution.py:301
  12.9 9.4 %collective-permute-start.5 = (f32[1,512,128]{2,1,0:T(8,128)S(1)}, f32[1,512,128]{2,1,0:T(8,128)S(1)}, u32[]{:S(2)}, u32[]{:S(2)}) collective-permute-start(f32[1,512,128]{2,1,0:T(8,128)S(1)} %get-tuple-element.28.own_kept), channel_id=1, source_target_pairs={{0,1},{1,0},{2,3},{3,2},{4,5},{5,4},{6,7},{7,6},{8,9},{9,8},{10,11... | collective-permute-start | bytes 786440 | tf_op jit(solution)/shard_map/ppermute | solution.py:301
  21.2 1.6 %collective-permute-start.6 = (f32[1,512,128]{2,1,0:T(8,128)S(1)}, f32[1,512,128]{2,1,0:T(8,128)S(1)}, u32[]{:S(2)}, u32[]{:S(2)}) collective-permute-start(f32[1,512,128]{2,1,0:T(8,128)S(1)} %shard_map.60.own_came), channel_id=1, source_target_pairs={{0,1},{1,0},{2,3},{3,2},{4,5},{5,4},{6,7},{7,6},{8,9},{9,8},{10,11... | collective-permute-start | bytes 786440 | tf_op jit(solution)/shard_map/ppermute | solution.py:301
  21.3 9.2 %collective-permute-start.4 = (f32[1,512,128]{2,1,0:T(8,128)S(1)}, f32[1,512,128]{2,1,0:T(8,128)S(1)}, u32[]{:S(2)}, u32[]{:S(2)}) collective-permute-start(f32[1,512,128]{2,1,0:T(8,128)S(1)} %get-tuple-element.27), channel_id=1, source_target_pairs={{0,2},{1,3},{2,0},{3,1},{4,6},{5,7},{6,4},{7,5},{8,10},{9,11},{10,... | collective-permute-start | bytes 786440 | tf_op jit(solution)/shard_map/ppermute | solution.py:301
  24.0 11.6 %collective-permute-start.7 = (f32[1,512,128]{2,1,0:T(8,128)S(1)}, f32[1,512,128]{2,1,0:T(8,128)S(1)}, u32[]{:S(2)}, u32[]{:S(2)}) collective-permute-start(f32[1,512,128]{2,1,0:T(8,128)S(1)} %get-tuple-element.32), channel_id=1, source_target_pairs={{0,2},{1,3},{2,0},{3,1},{4,6},{5,7},{6,4},{7,5},{8,10},{9,11},{10,... | collective-permute-start | bytes 786440 | tf_op jit(solution)/shard_map/ppermute | solution.py:301
where the time goes:
time: 37.3 us; the launch traced here: 37.1 us
  Pallas kernels  15.8 us (42%)
  waiting for transfers between devices  13.7 us (37%)
  starting transfers between devices  6.39 us (17%)
  local copies, waits for them, and re-layouts  1.09 us (3%)
    ppermute x8, waiting for transfers between devices, other(): return lax.ppermute(v, 'qa', [(i, i ^ bit) for i in range(devices)])  13.7 us
    pallas_call x7, Pallas kernels, call(): pl.pallas_call(body, out_shape=outs, in_specs=specs, out_specs=[VM] * len...  12.8 us
    ppermute x8, starting transfers between devices, other(): return lax.ppermute(v, 'qa', [(i, i ^ bit) for i in range(devices)])  6.39 us
    pallas_call x2, Pallas kernels, finish(): pl.pallas_call(last_kernel, out_shape=shape, grid=(2,), in_specs=[SM, VM,...  3.02 us
    dynamic_slice x1, local copies, waits for them, and re-layouts, block_of(): return lax.dynamic_slice_in_dim(v, (1 - h1) * 2 + c, 1, axis=0)  1.06 us
  transfers between devices with their start and end apart: 8, of which 4 were waited for; matrix products, arithmetic and copies ran while one was open for 0% of the time, Pallas kernels for 39%

commit v1 on v0

--- a/solution.py
+++ b/solution.py
@@ -100,41 +100,68 @@
     return lax.rem(me, 2), lax.rem(lax.div(me, 2), 2)
 
 
-def compose(first, count, flip, order, starts, unit, m_re, m_im):
+def halves(gdim, start):
+    if start == 0:
+        return [pl.ds(b * gdim, gdim) for b in range(2)]
+    return [pl.ds(b, gdim, stride=2) for b in range(2)]
+
+
+def begin(k, flip, order, starts, unit, m):
     gdim = unit.shape[-1]
-    row = lax.broadcasted_iota(jnp.int32, (2 * gdim, 2 * gdim), 0)
-    col = lax.broadcasted_iota(jnp.int32, (2 * gdim, 2 * gdim), 1)
-    one = jnp.where(row == jnp.bitwise_xor(col, flip), 1.0, 0.0).astype(F32)
-    for j in range(2):
-        m_re[j] = one[:, j * gdim : (j + 1) * gdim]
-    m_im[...] = jnp.zeros_like(m_im)
-
-    def step(k, carry):
-        gate = order[k]
-        w_hi, w_lo = split(embed(unit[gate, 0], unit[gate, 1]))
-
-        def run(rows):
-            blocks = [(j, r) for r in rows for j in range(2)]
+    gate, off = order[k], starts[k]
+    row = lax.broadcasted_iota(jnp.int32, (gdim, 2 * gdim), 0)
+    col = jnp.bitwise_xor(lax.broadcasted_iota(jnp.int32, (gdim, 2 * gdim), 1), flip)
+    ones = jnp.concatenate(
+        [
+            jnp.where(row * (1 + off) + b * (gdim - off * (gdim - 1)) == col, 1.0, 0.0)
+            for b in range(2)
+        ],
+        axis=1,
+    ).astype(BF16)
+    w_hi, w_lo = split(jnp.concatenate([unit[gate, 0], unit[gate, 1]], axis=0))
+    y = jnp.dot(
+        jnp.concatenate([w_hi, w_lo], axis=1),
+        jnp.concatenate([ones, ones], axis=0),
+        preferred_element_type=F32,
+    )
+    for start in range(2):
+
+        @pl.when(off == start)
+        def _():
+            store(m, [(r, j) for r in halves(gdim, start) for j in range(2)], y)
+
+
+def store(m, blocks, y):
+    gdim = y.shape[0] // 2
+    for i, (r, j) in enumerate(blocks):
+        for p in range(2):
+            m[p][j, r, :] = y[p * gdim : (p + 1) * gdim, gdim * i : gdim * (i + 1)]
+
+
+def apply(k, order, starts, unit, source, m):
+    gdim = unit.shape[-1]
+    gate = order[k]
+    w_hi, w_lo = split(embed(unit[gate, 0], unit[gate, 1]))
+    for start in range(2):
+
+        @pl.when(starts[k] == start)
+        def _():
+            blocks = [(r, j) for r in halves(gdim, start) for j in range(2)]
             x = jnp.concatenate(
-                [jnp.concatenate([m_re[j, r, :], m_im[j, r, :]], axis=0) for j, r in blocks],
+                [jnp.concatenate([v[j, r, :] for v in source], axis=0) for r, j in blocks],
                 axis=1,
             )
-            y = dot3(w_hi, w_lo, x)
-            for i, (j, r) in enumerate(blocks):
-                m_re[j, r, :] = y[:gdim, gdim * i : gdim * (i + 1)]
-                m_im[j, r, :] = y[gdim:, gdim * i : gdim * (i + 1)]
-
-        @pl.when(starts[k] == 0)
-        def _():
-            run([pl.ds(b * gdim, gdim) for b in range(2)])
-
-        @pl.when(starts[k] != 0)
-        def _():
-            run([pl.ds(b, gdim, stride=2) for b in range(2)])
-
+            store(m, blocks, dot3(w_hi, w_lo, x))
+
+
+def compose(first, count, flip, order, starts, unit, m):
+    begin(first, flip, order, starts, unit, m)
+
+    def step(k, carry):
+        apply(k, order, starts, unit, m, m)
         return carry
 
-    lax.fori_loop(first, first + count, step, 0)
+    lax.fori_loop(first + 1, first + count, step, 0)
 
 
 def put(ref, re, im):
@@ -151,31 +178,20 @@
     )
 
 
-def front_kernel(count, order, starts, unit, state, w_ref, kept0, kept1, m_re, m_im, u, s, sems):
-    _, h1 = my_bits()
-    copies = [
-        pltpu.make_async_copy(unit, u, sems.at[0]),
-        pltpu.make_async_copy(state.at[pl.ds(h1 * 2, 2)], s, sems.at[1]),
-    ]
-    for c in copies:
-        c.start()
-    copies[0].wait()
-    compose(0, count, 0, order, starts, u, m_re, m_im)
-    put(w_ref, whole(m_re), whole(m_im))
-    copies[1].wait()
-    rows = s.shape[1] // 2
-    x = jnp.concatenate([parts_of(s, c, rows) for c in range(2)], axis=1)
-    y = dot3(w_ref[0], w_ref[1], x)
-    lanes = s.shape[2]
-    kept0[0] = y[:, :lanes]
-    kept1[0] = y[:, lanes:]
-
-
-def second_kernel(count, order, starts, pair, unit, w_ref, m_re, m_im):
+def front_kernel(count, order, starts, pair, unit, w0_ref, w1_ref, re_ref, im_ref, *scratch):
+    order_s, starts_s, u, m_re, m_im, sems = scratch
     gdim = unit.shape[-1]
     half = gdim // 2
     h0, h1 = my_bits()
-    compose(count, count, h1 * gdim + h0 * half, order, starts, unit, m_re, m_im)
+    pairs = ((order, order_s), (starts, starts_s), (unit, u))
+    copies = [pltpu.make_async_copy(a, b, sems.at[i]) for i, (a, b) in enumerate(pairs)]
+    for c in copies:
+        c.start()
+    for c in copies:
+        c.wait()
+    compose(0, count, 0, order_s, starts_s, u, (m_re, m_im))
+    put(w0_ref, whole(m_re), whole(m_im))
+    compose(count, count, h1 * gdim + h0 * half, order_s, starts_s, u, (m_re, m_im))
     re, im = [], []
     for k in range(2):
         at = lax.rem(h1 + k, 2) * gdim
@@ -190,29 +206,51 @@
             i += v_re * x_im + v_im * x_re
         re.append(r)
         im.append(i)
-    put(w_ref, jnp.concatenate(re, axis=0), jnp.concatenate(im, axis=0))
-
-
-def third_kernel(count, order, starts, unit, w_ref, m_re, m_im):
-    compose(2 * count, count, 0, order, starts, unit, m_re, m_im)
-    put(w_ref, whole(m_re), whole(m_im))
-
-
-def first_kernel(w_ref, raw, out):
-    rows = raw.shape[1] // 2
-    out[0] = dot3(w_ref[0], w_ref[1], parts_of(raw, 0, rows))
-
-
-def middle_kernel(w1_ref, w2_ref, own_kept, other_kept, own_came, other_came, keep, back):
-    lanes = own_kept.shape[2]
-    dim = own_kept.shape[1] // 2
+    put(w1_ref, jnp.concatenate(re, axis=0), jnp.concatenate(im, axis=0))
+    compose(2 * count, count // 2, 0, order_s, starts_s, u, (re_ref, im_ref))
+
+
+def third_kernel(count, order, starts, unit, re, im, w_ref, m_re, m_im):
+    m = (m_re, m_im)
+    source = (re, im)
+    for k in range(2 * count + count // 2, 3 * count):
+        apply(k, order, starts, unit, source, m)
+        source = m
+    put(w_ref, whole(source[0]), whole(source[1]))
+
+
+def kept_kernel(chunk, w_ref, state, out):
+    _, h1 = my_bits()
+    rows = state.shape[1] // 2
+    out[0] = dot3(w_ref[0], w_ref[1], parts_of(state, h1 * 2 + chunk, rows))
+
+
+def came_kernel(w_ref, raw, out):
+    out[0] = dot3(w_ref[0], w_ref[1], parts_of(raw, 0, raw.shape[1] // 2))
+
+
+def enter_kernel(chunk, w_ref, state, raw, out):
+    _, h1 = my_bits()
+    rows, lanes = raw.shape[1] // 2, raw.shape[2]
+    x = jnp.concatenate([parts_of(state, h1 * 2 + chunk, rows), parts_of(raw, 0, rows)], axis=1)
+    y = dot3(w_ref[0], w_ref[1], x)
+    out[0] = y[:, :lanes]
+    out[1] = y[:, lanes:]
+
+
+def middle_kernel(count, w1_ref, w2_ref, *refs):
+    blocks, (keep, back) = refs[:count], refs[count:]
+    lanes = back.shape[2]
+    dim = back.shape[1] // 2
     part = dim // 4
-    sources = (own_kept, other_kept, own_came, other_came)
+    sources = [(v, k) for v in blocks for k in range(v.shape[0])]
+    if count == 2:
+        sources = [sources[0], sources[2], sources[1], sources[3]]
     cols = []
     for f in range(4):
         cols.append(
             jnp.concatenate(
-                [s[0, pl.ds(p * dim + f * part, part), :] for p in range(2) for s in sources],
+                [v[k, pl.ds(p * dim + f * part, part), :] for p in range(2) for v, k in sources],
                 axis=0,
             )
         )
@@ -234,17 +272,40 @@
     back[0] = z[:, lanes:]
 
 
-def last_kernel(pair, keep, back, *refs):
-    out = refs[-1]
+def scale_kernel(pair, keep, part0, part1, coef):
     _, h1 = my_bits()
-    b = pl.program_id(0)
-    rows = keep.shape[1] // 2
-    k_re, k_im = keep[0, :rows, :], keep[0, rows:, :]
-    b_re, b_im = back[0, :rows, :], back[0, rows:, :]
-    v_re, v_im = pair[0, 0, b, h1], pair[0, 1, b, h1]
-    u_re, u_im = pair[0, 0, b, 1 - h1], pair[0, 1, b, 1 - h1]
-    out[0, 0, pl.ds(0, rows, stride=2), :] = v_re * k_re - v_im * k_im + u_re * b_re - u_im * b_im
-    out[0, 0, pl.ds(1, rows, stride=2), :] = v_re * k_im + v_im * k_re + u_re * b_im + u_im * b_re
+    dim = keep.shape[1] // 2
+    k_re, k_im = keep[0, :dim, :], keep[0, dim:, :]
+    for b, out in enumerate((part0, part1)):
+        v_re, v_im = pair[0, 0, b, h1], pair[0, 1, b, h1]
+        out[0, :dim, :] = v_re * k_re - v_im * k_im
+        out[0, dim:, :] = v_re * k_im + v_im * k_re
+        for p in range(2):
+            coef[b, p] = jnp.full(coef.shape[2:], pair[0, p, b, 1 - h1], F32)
+
+
+def last_kernel(chunk, part0, part1, back, coef, *refs):
+    out, buf, sems = refs[-3:]
+    rows = back.shape[1] // 2
+    cut = rows // 2
+    copies = []
+    for b, part in enumerate((part0, part1)):
+        for q in range(2):
+            at = q * cut
+            u_re, u_im = coef[b, 0][:1], coef[b, 1][:1]
+            re, im = pl.ds(at, cut), pl.ds(rows + at, cut)
+            b_re, b_im = back[0, re, :], back[0, im, :]
+            buf[b, pl.ds(2 * at, cut, stride=2), :] = part[0, re, :] + (u_re * b_re - u_im * b_im)
+            buf[b, pl.ds(2 * at + 1, cut, stride=2), :] = part[0, im, :] + (u_re * b_im + u_im * b_re)
+            span = pl.ds(2 * at, 2 * cut)
+            copies.append(
+                pltpu.make_async_copy(
+                    buf.at[b, span], out.at[b, chunk, span], sems.at[2 * b + q]
+                )
+            )
+            copies[-1].start()
+    for c in copies:
+        c.wait()
 
 
 VM = pl.BlockSpec(memory_space=pltpu.VMEM)
@@ -272,16 +333,16 @@
     )(*args)
 
 
-def finish(pair, keep, back, shape, chunk, before=None):
-    args = [pair, keep, back] + ([] if before is None else [before])
+def finish(args, shape, chunk, before=None):
+    args = args + ([] if before is None else [before])
     return pl.pallas_call(
-        last_kernel,
+        partial(last_kernel, chunk),
         out_shape=shape,
-        grid=(2,),
-        in_specs=[SM, VM, VM] + ([] if before is None else [HB]),
-        out_specs=pl.BlockSpec((1, 1, *shape.shape[2:]), lambda i: (i, chunk, 0, 0)),
-        input_output_aliases={} if before is None else {3: 0},
-        cost_estimate=cost([shape], [keep, back], 0),
+        in_specs=[VM] * 4 + [HB] * (len(args) - 4),
+        out_specs=HB,
+        input_output_aliases={} if before is None else {4: 0},
+        scratch_shapes=[pltpu.VMEM((2, *shape.shape[2:]), F32), pltpu.SemaphoreType.DMA((4,))],
+        cost_estimate=cost([shape], args[:3], 0),
         compiler_params=PARAMS,
     )(*args)
 
@@ -305,65 +366,63 @@
 
     view = state.reshape(2, -1, lanes).transpose(1, 0, 2).reshape(4, rows, lanes)
     came = [other(block_of(view, c), 2) for c in range(2)]
-    scratch = [pltpu.VMEM((2, dim, gdim), F32)] * 2
     step = 3 * 2 * (2 * gdim) * (2 * gdim) * (4 * gdim)
-    block = f32((1, rows, lanes))
-    w0, *kept = call(
+    enter_flops = 6 * rows * rows * lanes
+    block, both, coef = f32((1, rows, lanes)), f32((2, rows, lanes)), f32((2, 2, 8, lanes))
+    m = f32((2, dim, gdim))
+    m_scratch = pltpu.VMEM(m.shape, F32)
+    gates = [gate_order, gate_starts]
+    w0, w1, re2, im2 = call(
         partial(front_kernel, count),
-        [bf16((2, rows, rows)), block, block],
-        [far(gate_order), far(gate_starts), far(unitaries), far(view)],
-        [SM, SM, HB, HB],
-        scratch
-        + [
-            pltpu.VMEM(unitaries.shape, F32),
-            pltpu.VMEM((2, rows, lanes), F32),
-            pltpu.SemaphoreType.DMA((2,)),
-        ],
-        flops=count * step + 6 * rows * rows * 2 * lanes,
-    )
-    kept_other = [other(k, 1) for k in kept]
-    (w1,) = call(
-        partial(second_kernel, count),
-        [bf16((2, dim, rows))],
-        [gate_order, gate_starts, pair, unitaries],
-        [SM, SM, SM, VM],
-        scratch,
-        flops=count * step,
-    )
-
-    def enter(v):
-        flops = 6 * rows * rows * lanes
-        return call(first_kernel, [block], [w0, v], [VM, VM], flops=flops)[0]
-
-    def middle(c, mine):
-        return call(
-            middle_kernel,
-            [block, block],
-            [w1, w2, kept[c], kept_other[c], mine, other(mine, 1)],
-            [VM] * 6,
-            flops=6 * rows * rows * 4 * lanes,
-        )
-
-    came[0], w1 = tie((came[0], w1))
-    mine = enter(came[0])
-    order_then, mine = tie((gate_order, mine))
+        [bf16((2, rows, rows)), bf16((2, dim, rows)), m, m],
+        [far(v) for v in (*gates, pair, unitaries)],
+        [HB, HB, SM, HB],
+        [pltpu.SMEM(gate_order.shape, jnp.int32)] * 2
+        + [pltpu.VMEM(unitaries.shape, F32), m_scratch, m_scratch, pltpu.SemaphoreType.DMA((3,))],
+        flops=5 * count * step // 2,
+    )
+    (kept,) = call(partial(kept_kernel, 0), [block], [w0, view], [VM] * 2, flops=enter_flops)
+    kept_other = other(kept, 1)
+    re2, kept = tie((re2, kept))
+    came[0], re2 = tie((came[0], re2))
+    (mine,) = call(came_kernel, [block], [w0, came[0]], [VM] * 2, flops=enter_flops)
+    re2, mine = tie((re2, mine))
     (w2,) = call(
         partial(third_kernel, count),
         [bf16((2, rows, rows))],
-        [order_then, gate_starts, unitaries],
-        [SM, SM, VM],
-        scratch,
-        flops=count * step,
-    )
-    keep0, back0 = middle(0, mine)
-    came[1], back0 = tie((came[1], back0))
+        [*gates, unitaries, re2, im2],
+        [SM] * 2 + [VM] * 3,
+        [m_scratch, m_scratch],
+        flops=count * step // 2,
+    )
+
+    def middle(blocks):
+        return call(
+            partial(middle_kernel, len(blocks)),
+            [block, block],
+            [w1, w2, *blocks],
+            [VM] * (2 + len(blocks)),
+            flops=4 * enter_flops,
+        )
+
+    def scale(keep):
+        return call(scale_kernel, [block, block, coef], [pair, keep], [SM, VM])
+
+    shape = f32((2, 2, rows, lanes))
+    keep0, back0 = middle([kept, kept_other, mine, other(mine, 1)])
     back0 = other(back0, 2)
-    keep1, back1 = middle(1, enter(came[1]))
+    (mine,) = call(
+        partial(enter_kernel, 1), [both], [w0, view, came[1]], [VM] * 3, flops=2 * enter_flops
+    )
+    theirs = other(mine, 1)
+    mine, keep0 = tie((mine, keep0))
+    keep0 = scale(keep0)
+    keep1, back1 = middle([mine, theirs])
     back0, keep1 = tie((back0, keep1))
     back1 = other(back1, 2)
-    whole_shape = f32((2, 2, rows, lanes))
-    out = finish(pair, keep0, back0, whole_shape, 0)
-    out = finish(pair, keep1, back1, whole_shape, 1, out)
+    *keep1, coef1 = scale(keep1)
+    out = finish([*keep0[:2], back0, keep0[2]], shape, 0)
+    out = finish([*keep1, back1, coef1], shape, 1, out)
     return out.reshape(-1, 2, lanes).transpose(1, 0, 2).reshape(2, -1)
 
 

time: 37.3 us -> 34.8 us (0.933)
  waiting for transfers between devices: 13.7 us -> 12.4 us
  Pallas kernels: 15.8 us -> 15 us
  starting transfers between devices: 6.39 us -> 5.97 us
    pallas_call x2, Pallas kernels: 3.02 us -> 1.68 us  [finish(): pl.pallas_call(partial(last_kernel, chunk), out_shape=shape, in_specs=[VM...]
    ppermute x8 -> x7, waiting for transfers between devices: 13.7 us -> 12.4 us  [other(): return lax.ppermute(v, 'qa', [(i, i ^ bit) for i in range(devices)])]
    pallas_call x7 -> x9, Pallas kernels: 12.8 us -> 13.3 us  [call(): pl.pallas_call(body, out_shape=outs, in_specs=specs, out_specs=[VM] * len...]
    ppermute x8 -> x7, starting transfers between devices: 6.39 us -> 5.97 us  [other(): return lax.ppermute(v, 'qa', [(i, i ^ bit) for i in range(devices)])]
  transfers between devices with their start and end apart: 8 -> 7, of which waited for: 4 -> 4; matrix products, arithmetic and copies ran while one was open for 0% -> 0% of each run, Pallas kernels for 39% -> 41%
where the time goes in v1:
time: 34.8 us; the launch traced here: 34.6 us
  Pallas kernels  15 us (43%)
  waiting for transfers between devices  12.4 us (36%)
  starting transfers between devices  5.97 us (17%)
  local copies, waits for them, and re-layouts  1.09 us (3%)
    pallas_call x9, Pallas kernels, call(): pl.pallas_call(body, out_shape=outs, in_specs=specs, out_specs=[VM] * len...  13.3 us
    ppermute x7, waiting for transfers between devices, other(): return lax.ppermute(v, 'qa', [(i, i ^ bit) for i in range(devices)])  12.4 us
    ppermute x7, starting transfers between devices, other(): return lax.ppermute(v, 'qa', [(i, i ^ bit) for i in range(devices)])  5.97 us
    pallas_call x2, Pallas kernels, finish(): pl.pallas_call(partial(last_kernel, chunk), out_shape=shape, in_specs=[VM...  1.68 us
    dynamic_slice x1, local copies, waits for them, and re-layouts, block_of(): return lax.dynamic_slice_in_dim(v, (1 - h1) * 2 + c, 1, axis=0)  1.06 us
  transfers between devices with their start and end apart: 7, of which 4 were waited for; matrix products, arithmetic and copies ran while one was open for 0% of the time, Pallas kernels for 41%

profile of v1, /device:TPU:0, one launch (start us, length us, event | category | flops | bytes accessed | tf_op | source)
XLA Modules:
  0.0 34.6 jit_solution(16584403115337981938)
XLA Ops:
  0.0 1.1 %constant_dynamic-slice_fusion = (f32[1,512,128]{2,1,0:T(8,128)S(1)}, f32[1,512,128]{2,1,0:T(8,128)S(1)}) fusion(f32[4,512,128]{2,1,0:T(8,128)} %bitcast.10, s32[]{:T(128)S(6)} %select_n.7, s32[]{:T(128)S(6)} %select_n.6), kind=kLoop, calls=%fused_computation | loop fusion | bytes 1048584 | tf_op jit(solution)/shard_map/dynamic_slice | solution.py:365
  1.1 3.0 %collective-permute-start.4 = (f32[1,512,128]{2,1,0:T(8,128)S(1)}, f32[1,512,128]{2,1,0:T(8,128)S(1)}, u32[]{:S(2)}, u32[]{:S(2)}) collective-permute-start(f32[1,512,128]{2,1,0:T(8,128)S(1)} %get-tuple-element.53), channel_id=1, source_target_pairs={{0,2},{1,3},{2,0},{3,1},{4,6},{5,7},{6,4},{7,5},{8,10},{9,11},{10,... | collective-permute-start | bytes 786440 | tf_op jit(solution)/shard_map/ppermute | solution.py:362
  4.1 0.0 copy-start
  4.1 0.1 collective-permute-start
  4.2 6.4 %shard_map.55 = (bf16[2,512,512]{2,1,0:T(8,128)(2,1)S(1)}, bf16[2,256,512]{2,1,0:T(8,128)(2,1)S(1)}, f32[2,256,128]{2,1,0:T(8,128)S(1)}, f32[2,256,128]{2,1,0:T(8,128)S(1)}) custom-call(s32[12]{0:T(128)} %order.3, s32[12]{0:T(128)} %starts.3, f32[2,2,2,2]{3,2,1,0:T(2,128)} %pair.5, f32[12,2,128,128]{3,2,1,0:T(8,128)} %unit.3), custom_call_target="tpu_custom_call" | custom-call | flops 2013265920 | bytes 3670176 | tf_op jit(solution)/shard_map/pallas_call | solution.py:325
  10.6 0.7 %collective-permute-done.4.raw = f32[1,512,128]{2,1,0:T(8,128)S(1)} collective-permute-done((f32[1,512,128]{2,1,0:T(8,128)S(1)}, f32[1,512,128]{2,1,0:T(8,128)S(1)}, u32[]{:S(2)}, u32[]{:S(2)}) %collective-permute-start.4) | collective-permute-done | bytes 262176 | tf_op jit(solution)/shard_map/ppermute | solution.py:362
  11.3 0.0 copy-done
  11.3 0.6 %shard_map.60.refs_0_ = f32[2,512,128]{2,1,0:T(8,128)S(1)} custom-call(bf16[2,512,512]{2,1,0:T(8,128)(2,1)S(1)} %get-tuple-element.31.w_ref, f32[4,512,128]{2,1,0:T(8,128)S(1)} %bitcast.11, f32[1,512,128]{2,1,0:T(8,128)S(1)} %collective-permute-done.4.raw), custom_call_target="tpu_custom_call" | custom-call | flops 402653184 | bytes 2883584 | tf_op jit(solution)/shard_map/pallas_call | solution.py:325
  11.8 0.0 copy-start.1
  11.9 0.0 copy-start.3
  11.9 0.0 copy-start.4
  11.9 0.1 collective-permute-start.5
  12.0 0.6 %shard_map.56.refs_0_ = f32[1,512,128]{2,1,0:T(8,128)S(1)} custom-call(bf16[2,512,512]{2,1,0:T(8,128)(2,1)S(1)} %get-tuple-element.31.w_ref, f32[4,512,128]{2,1,0:T(8,128)S(1)} %bitcast.12), custom_call_target="tpu_custom_call" | custom-call | flops 201326592 | bytes 2359296 | tf_op jit(solution)/shard_map/pallas_call | solution.py:325
  12.6 0.5 %collective-permute-start.1 = (f32[1,512,128]{2,1,0:T(8,128)S(1)}, f32[1,512,128]{2,1,0:T(8,128)S(1)}, u32[]{:S(2)}, u32[]{:S(2)}) collective-permute-start(f32[1,512,128]{2,1,0:T(8,128)S(1)} %shard_map.56.refs_0_), channel_id=1, source_target_pairs={{0,1},{1,0},{2,3},{3,2},{4,5},{5,4},{6,7},{7,6},{8,9},{9,8},{10,11... | collective-permute-start | bytes 786440 | tf_op jit(solution)/shard_map/ppermute | solution.py:362
  13.1 2.9 %collective-permute-done.raw = f32[1,512,128]{2,1,0:T(8,128)S(1)} collective-permute-done((f32[1,512,128]{2,1,0:T(8,128)S(1)}, f32[1,512,128]{2,1,0:T(8,128)S(1)}, u32[]{:S(2)}, u32[]{:S(2)}) %collective-permute-start) | collective-permute-done | bytes 262176 | tf_op jit(solution)/shard_map/ppermute | solution.py:362
  16.0 0.6 %shard_map.57.refs_2_ = f32[1,512,128]{2,1,0:T(8,128)S(1)} custom-call(bf16[2,512,512]{2,1,0:T(8,128)(2,1)S(1)} %get-tuple-element.31.w_ref, f32[1,512,128]{2,1,0:T(8,128)S(1)} %collective-permute-done.raw), custom_call_target="tpu_custom_call" | custom-call | flops 201326592 | bytes 1572864 | tf_op jit(solution)/shard_map/pallas_call | solution.py:325
  16.6 0.1 collective-permute-start.2
  16.7 0.0 copy-done.1
  16.7 0.0 copy-done.3
  16.7 0.0 copy-done.4
  16.7 1.5 %shard_map.58.w2_ref = bf16[2,512,512]{2,1,0:T(8,128)(2,1)S(1)} custom-call(s32[12]{0:T(128)S(1)} %copy-done.3, s32[12]{0:T(128)S(1)} %copy-done.4, f32[12,2,128,128]{3,2,1,0:T(8,128)S(1)} %copy-done.1, f32[2,256,128]{2,1,0:T(8,128)S(1)} %get-tuple-element.35.re, f32[2,256,128]{2,1,0:T(8,128)S(1)} %get-tuple-element.36.im), custom_call_target="tpu_custom_call" | custom-call | flops 402653184 | bytes 3145824 | tf_op jit(solution)/shard_map/pallas_call | solution.py:325
  18.2 0.0 collective-permute-done.1.refs_1_
  18.2 0.0 collective-permute-done.2.refs_3_
  18.3 1.1 %shard_map.59 = (f32[1,512,128]{2,1,0:T(8,128)S(1)}, f32[1,512,128]{2,1,0:T(8,128)S(1)}) custom-call(bf16[2,256,512]{2,1,0:T(8,128)(2,1)S(1)} %get-tuple-element.29.w1_ref, bf16[2,512,512]{2,1,0:T(8,128)(2,1)S(1)} %shard_map.58.w2_ref, f32[1,512,128]{2,1,0:T(8,128)S(1)} %shard_map.56.refs_0_, f32[1,512,128]{2,1,0:T(8,128)S(1)} %collective-permute-done.1.refs_1_, ...), custom_call_target="tpu_custom_call" | custom-call | flops 805306368 | bytes 3145728 | tf_op jit(solution)/shard_map/pallas_call | solution.py:325
  19.4 0.0 copy-start.2
  19.4 1.8 %collective-permute-start.3 = (f32[1,512,128]{2,1,0:T(8,128)S(1)}, f32[1,512,128]{2,1,0:T(8,128)S(1)}, u32[]{:S(2)}, u32[]{:S(2)}) collective-permute-start(f32[1,512,128]{2,1,0:T(8,128)S(1)} %get-tuple-element.39), channel_id=1, source_target_pairs={{0,2},{1,3},{2,0},{3,1},{4,6},{5,7},{6,4},{7,5},{8,10},{9,11},{10,... | collective-permute-start | bytes 786440 | tf_op jit(solution)/shard_map/ppermute | solution.py:362
  21.2 0.0 collective-permute-done.5.refs_1_
  21.2 1.1 %shard_map.61 = (f32[1,512,128]{2,1,0:T(8,128)S(1)}, f32[1,512,128]{2,1,0:T(8,128)S(1)}) custom-call(bf16[2,256,512]{2,1,0:T(8,128)(2,1)S(1)} %get-tuple-element.29.w1_ref, bf16[2,512,512]{2,1,0:T(8,128)(2,1)S(1)} %shard_map.58.w2_ref, f32[2,512,128]{2,1,0:T(8,128)S(1)} %shard_map.60.refs_0_, f32[2,512,128]{2,1,0:T(8,128)S(1)} %collective-permute-done.5.refs_1_), custom_call_target="tpu_custom_call" | custom-call | flops 805306368 | bytes 3145728 | tf_op jit(solution)/shard_map/pallas_call | solution.py:325
  22.4 0.3 %collective-permute-start.6 = (f32[1,512,128]{2,1,0:T(8,128)S(1)}, f32[1,512,128]{2,1,0:T(8,128)S(1)}, u32[]{:S(2)}, u32[]{:S(2)}) collective-permute-start(f32[1,512,128]{2,1,0:T(8,128)S(1)} %get-tuple-element.46), channel_id=1, source_target_pairs={{0,2},{1,3},{2,0},{3,1},{4,6},{5,7},{6,4},{7,5},{8,10},{9,11},{10,... | collective-permute-start | bytes 786440 | tf_op jit(solution)/shard_map/ppermute | solution.py:362
  22.7 0.0 copy-done.2
  22.7 0.7 %shard_map.63 = (f32[1,512,128]{2,1,0:T(8,128)S(1)}, f32[1,512,128]{2,1,0:T(8,128)S(1)}, f32[2,2,8,128]{3,2,1,0:T(8,128)S(1)}) custom-call(f32[2,2,2,2]{3,2,1,0:T(2,128)S(1)} %copy-done.2, f32[1,512,128]{2,1,0:T(8,128)S(1)} %get-tuple-element.48.keep), custom_call_target="tpu_custom_call" | custom-call | bytes 802880 | tf_op jit(solution)/shard_map/pallas_call | solution.py:325
  23.4 5.2 %collective-permute-done.3.back = f32[1,512,128]{2,1,0:T(8,128)S(1)} collective-permute-done((f32[1,512,128]{2,1,0:T(8,128)S(1)}, f32[1,512,128]{2,1,0:T(8,128)S(1)}, u32[]{:S(2)}, u32[]{:S(2)}) %collective-permute-start.3) | collective-permute-done | bytes 262176 | tf_op jit(solution)/shard_map/ppermute | solution.py:362
  28.7 0.7 %shard_map.62 = (f32[1,512,128]{2,1,0:T(8,128)S(1)}, f32[1,512,128]{2,1,0:T(8,128)S(1)}, f32[2,2,8,128]{3,2,1,0:T(8,128)S(1)}) custom-call(f32[2,2,2,2]{3,2,1,0:T(2,128)S(1)} %copy-done.2, f32[1,512,128]{2,1,0:T(8,128)S(1)} %get-tuple-element.43.keep), custom_call_target="tpu_custom_call" | custom-call | bytes 802880 | tf_op jit(solution)/shard_map/pallas_call | solution.py:325
  29.4 0.8 %shard_map.64.refs_0_ = f32[2,2,512,128]{3,2,1,0:T(8,128)} custom-call(f32[1,512,128]{2,1,0:T(8,128)S(1)} %get-tuple-element.49.part0, f32[1,512,128]{2,1,0:T(8,128)S(1)} %get-tuple-element.50.part1, f32[1,512,128]{2,1,0:T(8,128)S(1)} %collective-permute-done.3.back, f32[2,2,8,128]{3,2,1,0:T(8,128)S(1)} %get-tuple-element.52.coef), custom_call_target="tpu_custom_call" | custom-call | bytes 1835008 | tf_op jit(solution)/shard_map/pallas_call | solution.py:338
  30.2 3.6 %collective-permute-done.6.back = f32[1,512,128]{2,1,0:T(8,128)S(1)} collective-permute-done((f32[1,512,128]{2,1,0:T(8,128)S(1)}, f32[1,512,128]{2,1,0:T(8,128)S(1)}, u32[]{:S(2)}, u32[]{:S(2)}) %collective-permute-start.6) | collective-permute-done | bytes 262176 | tf_op jit(solution)/shard_map/ppermute | solution.py:362
  33.8 0.8 %shard_map.65 = f32[2,2,512,128]{3,2,1,0:T(8,128)} custom-call(f32[1,512,128]{2,1,0:T(8,128)S(1)} %get-tuple-element.44.part0, f32[1,512,128]{2,1,0:T(8,128)S(1)} %get-tuple-element.45.part1, f32[1,512,128]{2,1,0:T(8,128)S(1)} %collective-permute-done.6.back, f32[2,2,8,128]{3,2,1,0:T(8,128)S(1)} %get-tuple-element.47.coef, ...), custom_call_target="tpu_custom_call", output_to_operand_aliasing={{}: (4, {})} | custom-call | bytes 1835008 | tf_op jit(solution)/shard_map/pallas_call | solution.py:338
Async XLA Ops:
  1.1 10.2 %collective-permute-start.4 = (f32[1,512,128]{2,1,0:T(8,128)S(1)}, f32[1,512,128]{2,1,0:T(8,128)S(1)}, u32[]{:S(2)}, u32[]{:S(2)}) collective-permute-start(f32[1,512,128]{2,1,0:T(8,128)S(1)} %get-tuple-element.53), channel_id=1, source_target_pairs={{0,2},{1,3},{2,0},{3,1},{4,6},{5,7},{6,4},{7,5},{8,10},{9,11},{10,... | collective-permute-start | bytes 786440 | tf_op jit(solution)/shard_map/ppermute | solution.py:362
  4.1 7.2 %copy-start = (f32[2,131072]{1,0:T(2,128)S(1)}, f32[2,131072]{1,0:T(2,128)}, u32[]{:S(2)}) copy-start(f32[2,131072]{1,0:T(2,128)} %param.5) | copy-start | bytes 3145732
  4.1 11.9 %collective-permute-start = (f32[1,512,128]{2,1,0:T(8,128)S(1)}, f32[1,512,128]{2,1,0:T(8,128)S(1)}, u32[]{:S(2)}, u32[]{:S(2)}) collective-permute-start(f32[1,512,128]{2,1,0:T(8,128)S(1)} %get-tuple-element.54), channel_id=1, source_target_pairs={{0,2},{1,3},{2,0},{3,1},{4,6},{5,7},{6,4},{7,5},{8,10},{9,11},{10,... | collective-permute-start | bytes 786440 | tf_op jit(solution)/shard_map/ppermute | solution.py:362
  11.8 4.8 %copy-start.1 = (f32[12,2,128,128]{3,2,1,0:T(8,128)S(1)}, f32[12,2,128,128]{3,2,1,0:T(8,128)}, u32[]{:S(2)}) copy-start(f32[12,2,128,128]{3,2,1,0:T(8,128)} %unit.3) | copy-start | bytes 4718596
  11.9 4.8 %copy-start.3 = (s32[12]{0:T(128)S(1)}, s32[12]{0:T(128)}, u32[]{:S(2)}) copy-start(s32[12]{0:T(128)} %order.3) | copy-start | bytes 148
  11.9 4.8 %copy-start.4 = (s32[12]{0:T(128)S(1)}, s32[12]{0:T(128)}, u32[]{:S(2)}) copy-start(s32[12]{0:T(128)} %starts.3) | copy-start | bytes 148
  11.9 9.3 %collective-permute-start.5 = (f32[2,512,128]{2,1,0:T(8,128)S(1)}, f32[2,512,128]{2,1,0:T(8,128)S(1)}, u32[]{:S(2)}, u32[]{:S(2)}) collective-permute-start(f32[2,512,128]{2,1,0:T(8,128)S(1)} %shard_map.60.refs_0_), channel_id=1, source_target_pairs={{0,1},{1,0},{2,3},{3,2},{4,5},{5,4},{6,7},{7,6},{8,9},{9,8},{10,11... | collective-permute-start | bytes 1572872 | tf_op jit(solution)/shard_map/ppermute | solution.py:362
  12.6 5.7 %collective-permute-start.1 = (f32[1,512,128]{2,1,0:T(8,128)S(1)}, f32[1,512,128]{2,1,0:T(8,128)S(1)}, u32[]{:S(2)}, u32[]{:S(2)}) collective-permute-start(f32[1,512,128]{2,1,0:T(8,128)S(1)} %shard_map.56.refs_0_), channel_id=1, source_target_pairs={{0,1},{1,0},{2,3},{3,2},{4,5},{5,4},{6,7},{7,6},{8,9},{9,8},{10,11... | collective-permute-start | bytes 786440 | tf_op jit(solution)/shard_map/ppermute | solution.py:362
  16.6 1.6 %collective-permute-start.2 = (f32[1,512,128]{2,1,0:T(8,128)S(1)}, f32[1,512,128]{2,1,0:T(8,128)S(1)}, u32[]{:S(2)}, u32[]{:S(2)}) collective-permute-start(f32[1,512,128]{2,1,0:T(8,128)S(1)} %shard_map.57.refs_2_), channel_id=1, source_target_pairs={{0,1},{1,0},{2,3},{3,2},{4,5},{5,4},{6,7},{7,6},{8,9},{9,8},{10,11... | collective-permute-start | bytes 786440 | tf_op jit(solution)/shard_map/ppermute | solution.py:362
  19.4 3.3 %copy-start.2 = (f32[2,2,2,2]{3,2,1,0:T(2,128)S(1)}, f32[2,2,2,2]{3,2,1,0:T(2,128)}, u32[]{:S(2)}) copy-start(f32[2,2,2,2]{3,2,1,0:T(2,128)} %pair.5) | copy-start | bytes 196
  19.4 9.2 %collective-permute-start.3 = (f32[1,512,128]{2,1,0:T(8,128)S(1)}, f32[1,512,128]{2,1,0:T(8,128)S(1)}, u32[]{:S(2)}, u32[]{:S(2)}) collective-permute-start(f32[1,512,128]{2,1,0:T(8,128)S(1)} %get-tuple-element.39), channel_id=1, source_target_pairs={{0,2},{1,3},{2,0},{3,1},{4,6},{5,7},{6,4},{7,5},{8,10},{9,11},{10,... | collective-permute-start | bytes 786440 | tf_op jit(solution)/shard_map/ppermute | solution.py:362
  22.4 11.4 %collective-permute-start.6 = (f32[1,512,128]{2,1,0:T(8,128)S(1)}, f32[1,512,128]{2,1,0:T(8,128)S(1)}, u32[]{:S(2)}, u32[]{:S(2)}) collective-permute-start(f32[1,512,128]{2,1,0:T(8,128)S(1)} %get-tuple-element.46), channel_id=1, source_target_pairs={{0,2},{1,3},{2,0},{3,1},{4,6},{5,7},{6,4},{7,5},{8,10},{9,11},{10,... | collective-permute-start | bytes 786440 | tf_op jit(solution)/shard_map/ppermute | solution.py:362

commit v2 on v1

v2 whole, which is shorter than its diff:
```python
from functools import partial

import jax
import jax.numpy as jnp
from jax import lax
from jax.experimental import pallas as pl
from jax.experimental.pallas import tpu as pltpu
from jax.sharding import PartitionSpec as P


HIGH = lax.Precision.HIGHEST
F32 = jnp.float32
BF16 = jnp.bfloat16


def mix(mat, vec):
    return jnp.einsum("ij,ajb->aib", mat, vec, precision=HIGH)


def dense_branch(re_part, im_part, u_re, u_im, offset):
    gdim = u_re.shape[0]
    gq = gdim.bit_length() - 1
    block = 2 ** (gq + offset)
    shaped_re = re_part.reshape(-1, gdim, block)
    shaped_im = im_part.reshape(-1, gdim, block)
    new_re = mix(u_re, shaped_re) - mix(u_im, shaped_im)
    new_im = mix(u_re, shaped_im) + mix(u_im, shaped_re)
    return (new_re.reshape(-1), new_im.reshape(-1))


def dense_gate(stacked, unitaries, gate_order, gate_starts, k):
    chosen = unitaries[gate_order[k]]
    branches = [partial(dense_branch, offset=0), partial(dense_branch, offset=1)]
    new_re, new_im = lax.switch(
        gate_starts[k], branches, stacked[0], stacked[1], chosen[0], chosen[1]
    )
    return jnp.stack([new_re, new_im])


def one_qubit(stacked, gate, qubit):
    shaped = stacked.reshape(2, -1, 2, 2**qubit)
    u_re, u_im = (gate[0], gate[1])
    new_re = jnp.einsum("bc,acx->abx", u_re, shaped[0], precision=HIGH) - jnp.einsum(
        "bc,acx->abx", u_im, shaped[1], precision=HIGH
    )
    new_im = jnp.einsum("bc,acx->abx", u_re, shaped[1], precision=HIGH) + jnp.einsum(
        "bc,acx->abx", u_im, shaped[0], precision=HIGH
    )
    return jnp.stack([new_re, new_im]).reshape(2, -1)


def swap_qubits(stacked):
    devices = lax.axis_size("qa")
    shaped = stacked.reshape(2, devices, -1)
    moved = lax.all_to_all(shaped, "qa", split_axis=1, concat_axis=1, tiled=True)
    return moved.reshape(2, -1)


def general(state, unitaries, gate_order, gate_starts, pair_gates):
    local_bits = state.shape[1].bit_length() - 1
    global_bits = lax.axis_size("qa").bit_length() - 1
    ngates = unitaries.shape[0]
    third = ngates // 3
    stacked = state
    for k in range(third):
        stacked = dense_gate(stacked, unitaries, gate_order, gate_starts, k)
    stacked = one_qubit(stacked, pair_gates[0], local_bits - 1)
    stacked = swap_qubits(stacked)
    for k in range(third, 2 * third):
        stacked = dense_gate(stacked, unitaries, gate_order, gate_starts, k)
    stacked = one_qubit(stacked, pair_gates[1], local_bits - global_bits)
    stacked = swap_qubits(stacked)
    for k in range(2 * third, ngates):
        stacked = dense_gate(stacked, unitaries, gate_order, gate_starts, k)
    return stacked


def split(x):
    hi = x.astype(BF16)
    return hi, (x - hi.astype(F32)).astype(BF16)


def dot3(w_hi, w_lo, x):
    x_hi, x_lo = split(x)
    return jnp.dot(
        jnp.concatenate([w_hi, w_hi, w_lo], axis=1),
        jnp.concatenate([x_hi, x_lo, x_hi], axis=0),
        preferred_element_type=F32,
    )


def dot_narrow(w_hi, w_lo, x):
    n = x.shape[1]
    beside = jnp.concatenate(split(x), axis=1)
    y = jnp.dot(
        jnp.concatenate([w_hi, w_lo], axis=1),
        jnp.concatenate([beside, beside], axis=0),
        preferred_element_type=F32,
    )
    return y[:, :n] + y[:, n:]


def embed(re, im):
    return jnp.concatenate(
        [jnp.concatenate([re, -im], axis=1), jnp.concatenate([im, re], axis=1)], axis=0
    )


def my_bits():
    me = lax.axis_index("qa")
    return lax.rem(me, 2), lax.rem(lax.div(me, 2), 2)


def halves(gdim, start):
    if start == 0:
        return [pl.ds(b * gdim, gdim) for b in range(2)]
    return [pl.ds(b, gdim, stride=2) for b in range(2)]


def begin(u_re, u_im, off, flip, m):
    gdim = u_re.shape[0]
    row = lax.broadcasted_iota(jnp.int32, (gdim, 2 * gdim), 0)
    col = jnp.bitwise_xor(lax.broadcasted_iota(jnp.int32, (gdim, 2 * gdim), 1), flip)
    ones = jnp.concatenate(
        [
            jnp.where(row * (1 + off) + b * (gdim - off * (gdim - 1)) == col, 1.0, 0.0)
            for b in range(2)
        ],
        axis=1,
    ).astype(BF16)
    w_hi, w_lo = split(jnp.concatenate([u_re, u_im], axis=0))
    y = jnp.dot(
        jnp.concatenate([w_hi, w_lo], axis=1),
        jnp.concatenate([ones, ones], axis=0),
        preferred_element_type=F32,
    )
    for start in range(2):

        @pl.when(off == start)
        def _():
            store(m, [(r, j) for r in halves(gdim, start) for j in range(2)], y)


def store(m, blocks, y):
    gdim = y.shape[0] // 2
    for i, (r, j) in enumerate(blocks):
        for p in range(2):
            m[p][j, r, :] = y[p * gdim : (p + 1) * gdim, gdim * i : gdim * (i + 1)]


def apply(u_re, u_im, off, source, m):
    gdim = u_re.shape[0]
    w_hi, w_lo = split(embed(u_re, u_im))
    for start in range(2):

        @pl.when(off == start)
        def _():
            blocks = [(r, j) for r in halves(gdim, start) for j in range(2)]
            x = jnp.concatenate(
                [jnp.concatenate([v[j, r, :] for v in source], axis=0) for r, j in blocks],
                axis=1,
            )
            store(m, blocks, dot3(w_hi, w_lo, x))


def compose(count, flip, gate, m):
    begin(*gate(0), flip, m)

    def step(i, carry):
        apply(*gate(i), m, m)
        return carry

    lax.fori_loop(1, count, step, 0)


def put(ref, re, im):
    for i, w in enumerate((re, im - re, -(re + im))):
        ref[0, i], ref[1, i] = split(w)


def times(w_ref, re, im, product):
    both, t_re, t_im = (
        product(w_ref[0, i], w_ref[1, i], x) for i, x in enumerate((re + im, re, im))
    )
    return both + t_im, both + t_re


def whole(m):
    return jnp.concatenate([m[j] for j in range(2)], axis=1)


def parts_of(ref, at):
    rows = ref.shape[1] // 2
    return ref[at, pl.ds(0, rows, stride=2), :], ref[at, pl.ds(1, rows, stride=2), :]


def front_kernel(order, starts, pair, unit, w0_ref, units, flags, coef, *scratch):
    order_s, starts_s, pair_s, u, m_re, m_im, small_sems, sems, late_sems = scratch
    ngates, later = unit.shape[0], units.shape[0]
    count = ngates - later
    h0, h1 = my_bits()
    smalls = [
        pltpu.make_async_copy(a, b, small_sems.at[i])
        for i, (a, b) in enumerate(((order, order_s), (starts, starts_s), (pair, pair_s)))
    ]
    for c in smalls:
        c.start()

    def fetch(g):
        return pltpu.make_async_copy(unit.at[g], u.at[g], sems.at[g])

    def late(k):
        return pltpu.make_async_copy(unit.at[order_s[count + k]], units.at[k], late_sems.at[k])

    for g in range(ngates):
        fetch(g).start()
    for c in smalls:
        c.wait()
    for k in range(later):
        late(k).start()

    def gate(i):
        g = order_s[i]
        fetch(g).wait()
        return u[g, 0], u[g, 1], starts_s[i]

    compose(count, 0, gate, (m_re, m_im))
    put(w0_ref, whole(m_re), whole(m_im))
    bits = starts_s[count]
    for k in range(1, later):
        bits += starts_s[count + k] * 2**k
    flags[...] = jnp.full(flags.shape, bits, jnp.int32)
    for b in range(2):
        for p in range(2):
            for i, v in enumerate((pair_s[0, p, b, h1], pair_s[0, p, b, 1 - h1], pair_s[1, p, h0, b])):
                coef[i, b, p] = jnp.full(coef.shape[3:], v, F32)
    for k in range(later):
        fetch(order_s[count + k]).wait()
        late(k).wait()


def chosen(units, flags):
    bits = jnp.max(flags[...])

    def gate(k):
        return units[k, 0], units[k, 1], jnp.bitwise_and(lax.shift_right_logical(bits, k), 1)

    return gate


def second_kernel(units, flags, coef, w1_ref, re_ref, im_ref, m_re, m_im):
    count = units.shape[0] // 2
    gdim = units.shape[-1]
    half = gdim // 2
    h0, h1 = my_bits()
    gate = chosen(units, flags)
    compose(count, h1 * gdim + h0 * half, gate, (m_re, m_im))
    for k in range(2):
        at = lax.rem(h1 + k, 2) * gdim
        r, i = 0.0, 0.0
        for b in range(2):
            rows = pl.ds(pl.multiple_of(at + b * half, half), half)
            v_re, v_im = coef[2, b, 0][:1, :1], coef[2, b, 1][:1, :1]
            x_re, x_im = (
                jnp.concatenate([m[j, rows, :] for j in range(2)], axis=1) for m in (m_re, m_im)
            )
            r += v_re * x_re - v_im * x_im
            i += v_re * x_im + v_im * x_re
        w1_ref[0, k], w1_ref[1, k] = split(embed(r, i))
    compose(count // 2, 0, lambda i: gate(count + i), (re_ref, im_ref))


def third_kernel(units, flags, re, im, w_ref, m_re, m_im):
    count = units.shape[0] // 2
    gate = chosen(units, flags)
    source = (re, im)
    for k in range(count + count // 2, 2 * count):
        apply(*gate(k), source, (m_re, m_im))
        source = (m_re, m_im)
    put(w_ref, whole(source[0]), whole(source[1]))


def kept_kernel(w_ref, state, out):
    _, h1 = my_bits()
    rows, lanes = state.shape[1] // 2, state.shape[2]
    blocks = [parts_of(state, h1 * 2 + c) for c in range(2)]
    y = times(w_ref, *(jnp.concatenate(v, axis=1) for v in zip(*blocks)), dot3)
    for k in range(2):
        for p in range(2):
            out[k, p * rows : (p + 1) * rows] = y[p][:, k * lanes : (k + 1) * lanes]


def came_kernel(w_ref, raw, out):
    rows = raw.shape[1] // 2
    out[0, :rows], out[0, rows:] = times(w_ref, *parts_of(raw, 0), dot_narrow)


def through(k, chunk, w1_ref, w2_ref, kept, kept_other, mine, theirs):
    lanes = mine.shape[2]
    dim = mine.shape[1] // 2
    part = dim // 4
    sources = ((kept, chunk), (kept_other, chunk), (mine, 0), (theirs, 0))
    cols = [
        jnp.concatenate(
            [v[i, p * dim + f * part : p * dim + (f + 1) * part, :] for p in range(2) for v, i in sources],
            axis=0,
        )
        for f in range(4)
    ]
    y = dot3(w1_ref[0, k], w1_ref[1, k], jnp.concatenate(cols, axis=1))
    x = (
        jnp.concatenate(
            [y[p * part : (p + 1) * part, f * lanes : (f + 1) * lanes] for f in range(4)], axis=0
        )
        for p in range(2)
    )
    return times(w2_ref, *x, dot_narrow)


def back_kernel(chunk, *refs):
    out = refs[-1]
    dim = out.shape[1] // 2
    out[0, :dim], out[0, dim:] = through(1, chunk, *refs[:-1])


def keep_kernel(chunk, coef, *refs):
    k_re, k_im = through(0, chunk, *refs[:-2])
    dim = k_re.shape[0]
    for b, out in enumerate(refs[-2:]):
        v_re, v_im = coef[0, b, 0][:1], coef[0, b, 1][:1]
        out[0, :dim, :] = v_re * k_re - v_im * k_im
        out[0, dim:, :] = v_re * k_im + v_im * k_re


def last_kernel(chunk, part0, part1, back, coef, *refs):
    out, buf, sems = refs[-3:]
    rows = back.shape[1] // 2
    cut = rows // 2
    copies = []
    for b, part in enumerate((part0, part1)):
        for q in range(2):
            at = q * cut
            u_re, u_im = coef[1, b, 0][:1], coef[1, b, 1][:1]
            re, im = pl.ds(at, cut), pl.ds(rows + at, cut)
            b_re, b_im = back[0, re, :], back[0, im, :]
            buf[b, pl.ds(2 * at, cut, stride=2), :] = part[0, re, :] + (u_re * b_re - u_im * b_im)
            buf[b, pl.ds(2 * at + 1, cut, stride=2), :] = part[0, im, :] + (u_re * b_im + u_im * b_re)
            span = pl.ds(2 * at, 2 * cut)
            copies.append(
                pltpu.make_async_copy(
                    buf.at[b, span], out.at[b, chunk, span], sems.at[2 * b + q]
                )
            )
            copies[-1].start()
    for c in copies:
        c.wait()


VM = pl.BlockSpec(memory_space=pltpu.VMEM)
SM = pl.BlockSpec(memory_space=pltpu.SMEM)
HB = pl.BlockSpec(memory_space=pltpu.HBM)


def cost(outs, args, flops):
    nbytes = sum(a.size * a.dtype.itemsize for a in (*outs, *args))
    return pl.CostEstimate(flops=flops, bytes_accessed=nbytes, transcendentals=0)


PARAMS = pltpu.CompilerParams(vmem_limit_bytes=16 * 2**20)


def call(body, outs, args, specs, scratch=(), flops=0):
    results = pl.pallas_call(
        body,
        out_shape=outs,
        in_specs=specs,
        out_specs=[VM] * len(outs),
        scratch_shapes=scratch,
        cost_estimate=cost(outs, args, flops),
        compiler_params=PARAMS,
    )(*args)
    return list(results)


def finish(args, shape, chunk, before=None):
    args = args + ([] if before is None else [before])
    return pl.pallas_call(
        partial(last_kernel, chunk),
        out_shape=shape,
        in_specs=[VM] * 4 + [HB] * (len(args) - 4),
        out_specs=HB,
        input_output_aliases={} if before is None else {4: 0},
        scratch_shapes=[pltpu.VMEM((2, *shape.shape[2:]), F32), pltpu.SemaphoreType.DMA((4,))],
        cost_estimate=cost([shape], args[:3], 0),
        compiler_params=PARAMS,
    )(*args)


def paired(state, unitaries, gate_order, gate_starts, pair):
    devices = lax.axis_size("qa")
    count = unitaries.shape[0] // 3
    gdim = unitaries.shape[-1]
    lanes, rows, dim, half = gdim, 4 * gdim, 2 * gdim, gdim
    f32 = partial(jax.ShapeDtypeStruct, dtype=F32)
    bf16 = partial(jax.ShapeDtypeStruct, dtype=BF16)
    tie = lax.optimization_barrier
    far = partial(pltpu.with_memory_space_constraint, memory_space=pltpu.HBM)
    _, h1 = my_bits()

    def other(v, bit):
        return lax.ppermute(v, "qa", [(i, i ^ bit) for i in range(devices)])

    def block_of(v, c):
        return lax.dynamic_slice_in_dim(v, (1 - h1) * 2 + c, 1, axis=0)

    view = state.reshape(2, -1, lanes).transpose(1, 0, 2).reshape(4, rows, lanes)
    came = [other(block_of(view, c), 2) for c in range(2)]
    step = 3 * 2 * (2 * gdim) * (2 * gdim) * (4 * gdim)
    enter_flops = 6 * rows * rows * lanes
    block, both = f32((1, rows, lanes)), f32((2, rows, lanes))
    m = f32((2, dim, gdim))
    m_scratch = pltpu.VMEM(m.shape, F32)
    small = [gate_order, gate_starts, pair]
    ngates = unitaries.shape[0]
    tile = (8, lanes)
    dma = pltpu.SemaphoreType.DMA
    w0, units, flags, coef = call(
        front_kernel,
        [
            bf16((2, 3, dim, dim)),
            f32((2 * count, *unitaries.shape[1:])),
            jax.ShapeDtypeStruct(tile, jnp.int32),
            f32((3, 2, 2, *tile)),
        ],
        [far(v) for v in (*small, unitaries)],
        [HB] * 4,
        [pltpu.SMEM(v.shape, v.dtype) for v in small]
        + [pltpu.VMEM(unitaries.shape, F32), m_scratch, m_scratch]
        + [dma((3,)), dma((ngates,)), dma((2 * count,))],
        flops=count * step,
    )
    w1, re2, im2 = call(
        second_kernel,
        [bf16((2, 2, half, rows)), m, m],
        [units, flags, coef],
        [VM] * 3,
        [m_scratch, m_scratch],
        flops=3 * count * step // 2,
    )
    (kept,) = call(kept_kernel, [both], [w0, view], [VM] * 2, flops=2 * enter_flops)
    kept_other = other(kept, 1)
    re2, kept = tie((re2, kept))
    came[0], re2 = tie((came[0], re2))
    (mine,) = call(came_kernel, [block], [w0, came[0]], [VM] * 2, flops=enter_flops)
    re2, mine = tie((re2, mine))
    (w2,) = call(
        third_kernel,
        [bf16((2, 3, dim, dim))],
        [units, flags, re2, im2],
        [VM] * 4,
        [m_scratch, m_scratch],
        flops=count * step // 2,
    )

    def rest(c, mine):
        theirs = other(mine, 1)
        blocks = [w1, w2, kept, kept_other, mine, theirs]
        (back,) = call(partial(back_kernel, c), [block], blocks, [VM] * 6, flops=2 * enter_flops)
        return blocks, other(back, 2)

    def keep(c, blocks):
        return call(
            partial(keep_kernel, c),
            [block, block],
            [coef, *blocks],
            [VM] * 7,
            flops=2 * enter_flops,
        )

    shape = f32((2, 2, rows, lanes))
    blocks0, back0 = rest(0, mine)
    (mine,) = call(came_kernel, [block], [w0, came[1]], [VM] * 2, flops=enter_flops)
    blocks1, back1 = rest(1, mine)
    blocks0[0], blocks1[4] = tie((blocks0[0], blocks1[4]))
    keep0 = keep(0, blocks0)
    keep1 = keep(1, blocks1)
    back0, keep1[0] = tie((back0, keep1[0]))
    out = finish([*keep0, back0, coef], shape, 0)
    out = finish([*keep1, back1, coef], shape, 1, out)
    return out.reshape(-1, 2, lanes).transpose(1, 0, 2).reshape(2, -1)


def meets_two(state, unitaries, devices):
    local_bits = state.shape[1].bit_length() - 1
    global_bits = devices.bit_length() - 1
    top = 2 * (unitaries.shape[-1].bit_length() - 1) + 1
    met = top - (local_bits - global_bits)
    return met == 2 and local_bits == top + 2 and global_bits >= 2


def shards(*args):
    if meets_two(args[0], args[1], lax.axis_size("qa")):
        return paired(*args)
    return general(*args)


def solution(mesh):
    placed = (P(None, ("cuts", "qa")), P(), P(), P(), P())
    return jax.shard_map(
        shards, mesh=mesh, in_specs=placed, out_specs=P(None, ("cuts", "qa")), check_vma=False
    )
```

time: 34.8 us -> 34.2 us (0.983)
  Pallas kernels: 15 us -> 12.6 us
  waiting for transfers between devices: 12.4 us -> 14.6 us
  starting transfers between devices: 5.97 us -> 5.56 us
    pallas_call x9 -> x10, Pallas kernels: 13.3 us -> 10.9 us  [call(): pl.pallas_call(body, out_shape=outs, in_specs=specs, out_specs=[VM] * len...]
    ppermute x7, waiting for transfers between devices: 12.4 us -> 14.6 us  [other(): return lax.ppermute(v, 'qa', [(i, i ^ bit) for i in range(devices)])]
    ppermute x7, starting transfers between devices: 5.97 us -> 5.56 us  [other(): return lax.ppermute(v, 'qa', [(i, i ^ bit) for i in range(devices)])]
  transfers between devices with their start and end apart: 7 -> 7, of which waited for: 4 -> 4; matrix products, arithmetic and copies ran while one was open for 0% -> 0% of each run, Pallas kernels for 41% -> 35%
where the time goes in v2:
time: 34.2 us; the launch traced here: 34 us
  waiting for transfers between devices  14.6 us (43%)
  Pallas kernels  12.6 us (37%)
  starting transfers between devices  5.56 us (16%)
  local copies, waits for them, and re-layouts  1.07 us (3%)
    ppermute x7, waiting for transfers between devices, other(): return lax.ppermute(v, 'qa', [(i, i ^ bit) for i in range(devices)])  14.6 us
    pallas_call x10, Pallas kernels, call(): pl.pallas_call(body, out_shape=outs, in_specs=specs, out_specs=[VM] * len...  10.9 us
    ppermute x7, starting transfers between devices, other(): return lax.ppermute(v, 'qa', [(i, i ^ bit) for i in range(devices)])  5.56 us
    pallas_call x2, Pallas kernels, finish(): pl.pallas_call(partial(last_kernel, chunk), out_shape=shape, in_specs=[VM...  1.68 us
    dynamic_slice x1, local copies, waits for them, and re-layouts, block_of(): return lax.dynamic_slice_in_dim(v, (1 - h1) * 2 + c, 1, axis=0)  1.06 us
  transfers between devices with their start and end apart: 7, of which 4 were waited for; matrix products, arithmetic and copies ran while one was open for 0% of the time, Pallas kernels for 35%

profile of v2, /device:TPU:0, one launch (start us, length us, event | category | flops | bytes accessed | tf_op | source)
XLA Modules:
  0.0 34.0 jit_solution(5712961226063699727)
XLA Ops:
  0.0 1.1 %constant_dynamic-slice_fusion = (f32[1,512,128]{2,1,0:T(8,128)S(1)}, f32[1,512,128]{2,1,0:T(8,128)S(1)}) fusion(f32[4,512,128]{2,1,0:T(8,128)} %bitcast.10, s32[]{:T(128)S(6)} %select_n.7, s32[]{:T(128)S(6)} %select_n.6), kind=kLoop, calls=%fused_computation | loop fusion | bytes 1048584 | tf_op jit(solution)/shard_map/dynamic_slice | solution.py:414
  1.1 0.0 copy-start
  1.1 3.0 %collective-permute-start = (f32[1,512,128]{2,1,0:T(8,128)S(1)}, f32[1,512,128]{2,1,0:T(8,128)S(1)}, u32[]{:S(2)}, u32[]{:S(2)}) collective-permute-start(f32[1,512,128]{2,1,0:T(8,128)S(1)} %get-tuple-element.48), channel_id=1, source_target_pairs={{0,2},{1,3},{2,0},{3,1},{4,6},{5,7},{6,4},{7,5},{8,10},{9,11},{10,... | collective-permute-start | bytes 786440 | tf_op jit(solution)/shard_map/ppermute | solution.py:411
  4.1 2.9 %shard_map.55 = (bf16[2,3,256,256]{3,2,1,0:T(8,128)(2,1)S(1)}, f32[8,2,128,128]{3,2,1,0:T(8,128)S(1)}, s32[8,128]{1,0:T(8,128)S(1)}, f32[3,2,2,8,128]{4,3,2,1,0:T(8,128)S(1)}) custom-call(s32[12]{0:T(128)} %order.1, s32[12]{0:T(128)} %starts.1, f32[2,2,2,2]{3,2,1,0:T(2,128)} %pair.1, f32[12,2,128,128]{3,2,1,0:T(8,128)} %unit.1), custom_call_target="tpu_custom_call" | custom-call | flops 805306368 | bytes 3461280 | tf_op jit(solution)/shard_map/pallas_call | solution.py:373
  7.0 0.0 copy-done
  7.0 0.5 %shard_map.57.refs_2_ = f32[2,512,128]{2,1,0:T(8,128)S(1)} custom-call(bf16[2,3,256,256]{3,2,1,0:T(8,128)(2,1)S(1)} %get-tuple-element.31.w_ref, f32[4,512,128]{2,1,0:T(8,128)S(1)} %bitcast.11), custom_call_target="tpu_custom_call" | custom-call | flops 402653184 | bytes 2359296 | tf_op jit(solution)/shard_map/pallas_call | solution.py:373
  7.6 0.1 collective-permute-start.1
  7.7 0.2 collective-permute-start.4
  7.8 2.5 %shard_map.56 = (bf16[2,2,128,512]{3,2,1,0:T(8,128)(2,1)S(1)}, f32[2,256,128]{2,1,0:T(8,128)S(1)}, f32[2,256,128]{2,1,0:T(8,128)S(1)}) custom-call(f32[8,2,128,128]{3,2,1,0:T(8,128)S(1)} %get-tuple-element.26.units, s32[8,128]{1,0:T(8,128)S(1)} %get-tuple-element.27.flags, f32[3,2,2,8,128]{4,3,2,1,0:T(8,128)S(1)} %get-tuple-element.28.coef), custom_call_target="tpu_custom_call" | custom-call | flops 1207959552 | bytes 2150400 | tf_op jit(solution)/shard_map/pallas_call | solution.py:373
  10.3 0.5 %collective-permute-done.raw = f32[1,512,128]{2,1,0:T(8,128)S(1)} collective-permute-done((f32[1,512,128]{2,1,0:T(8,128)S(1)}, f32[1,512,128]{2,1,0:T(8,128)S(1)}, u32[]{:S(2)}, u32[]{:S(2)}) %collective-permute-start) | collective-permute-done | bytes 262176 | tf_op jit(solution)/shard_map/ppermute | solution.py:411
  10.8 0.4 %shard_map.58.refs_4_ = f32[1,512,128]{2,1,0:T(8,128)S(1)} custom-call(bf16[2,3,256,256]{3,2,1,0:T(8,128)(2,1)S(1)} %get-tuple-element.31.w_ref, f32[1,512,128]{2,1,0:T(8,128)S(1)} %collective-permute-done.raw), custom_call_target="tpu_custom_call" | custom-call | flops 201326592 | bytes 1310720 | tf_op jit(solution)/shard_map/pallas_call | solution.py:373
  11.2 0.1 collective-permute-start.2
  11.3 5.1 %collective-permute-done.4.raw = f32[1,512,128]{2,1,0:T(8,128)S(1)} collective-permute-done((f32[1,512,128]{2,1,0:T(8,128)S(1)}, f32[1,512,128]{2,1,0:T(8,128)S(1)}, u32[]{:S(2)}, u32[]{:S(2)}) %collective-permute-start.4) | collective-permute-done | bytes 262176 | tf_op jit(solution)/shard_map/ppermute | solution.py:411
  16.4 0.4 %shard_map.61.refs_4_ = f32[1,512,128]{2,1,0:T(8,128)S(1)} custom-call(bf16[2,3,256,256]{3,2,1,0:T(8,128)(2,1)S(1)} %get-tuple-element.31.w_ref, f32[1,512,128]{2,1,0:T(8,128)S(1)} %collective-permute-done.4.raw), custom_call_target="tpu_custom_call" | custom-call | flops 201326592 | bytes 1310720 | tf_op jit(solution)/shard_map/pallas_call | solution.py:373
  16.7 0.1 collective-permute-start.5
  16.8 1.1 %shard_map.59.refs_1_ = bf16[2,3,256,256]{3,2,1,0:T(8,128)(2,1)S(1)} custom-call(f32[8,2,128,128]{3,2,1,0:T(8,128)S(1)} %get-tuple-element.26.units, s32[8,128]{1,0:T(8,128)S(1)} %get-tuple-element.27.flags, f32[2,256,128]{2,1,0:T(8,128)S(1)} %get-tuple-element.35.re, f32[2,256,128]{2,1,0:T(8,128)S(1)} %get-tuple-element.36.im), custom_call_target="tpu_custom_call" | custom-call | flops 402653184 | bytes 2363392 | tf_op jit(solution)/shard_map/pallas_call | solution.py:373
  18.0 0.0 collective-permute-done.1.refs_3_
  18.0 0.0 collective-permute-done.2.refs_5_
  18.0 0.8 %shard_map.60 = f32[1,512,128]{2,1,0:T(8,128)S(1)} custom-call(bf16[2,2,128,512]{3,2,1,0:T(8,128)(2,1)S(1)} %get-tuple-element.43.refs_0_, bf16[2,3,256,256]{3,2,1,0:T(8,128)(2,1)S(1)} %shard_map.59.refs_1_, f32[2,512,128]{2,1,0:T(8,128)S(1)} %shard_map.57.refs_2_, f32[2,512,128]{2,1,0:T(8,128)S(1)} %collective-permute-done.1.refs_3_, ...), custom_call_target="tpu_custom_call" | custom-call | flops 402653184 | bytes 3145728 | tf_op jit(solution)/shard_map/pallas_call | solution.py:373
  18.8 1.5 %collective-permute-start.3 = (f32[1,512,128]{2,1,0:T(8,128)S(1)}, f32[1,512,128]{2,1,0:T(8,128)S(1)}, u32[]{:S(2)}, u32[]{:S(2)}) collective-permute-start(f32[1,512,128]{2,1,0:T(8,128)S(1)} %shard_map.60), channel_id=1, source_target_pairs={{0,2},{1,3},{2,0},{3,1},{4,6},{5,7},{6,4},{7,5},{8,10},{9,11},{10,... | collective-permute-start | bytes 786440 | tf_op jit(solution)/shard_map/ppermute | solution.py:411
  20.3 0.0 collective-permute-done.5.refs_5_
  20.3 0.8 %shard_map.63 = f32[1,512,128]{2,1,0:T(8,128)S(1)} custom-call(bf16[2,2,128,512]{3,2,1,0:T(8,128)(2,1)S(1)} %get-tuple-element.43.refs_0_, bf16[2,3,256,256]{3,2,1,0:T(8,128)(2,1)S(1)} %shard_map.59.refs_1_, f32[2,512,128]{2,1,0:T(8,128)S(1)} %shard_map.57.refs_2_, f32[2,512,128]{2,1,0:T(8,128)S(1)} %collective-permute-done.1.refs_3_, ...), custom_call_target="tpu_custom_call" | custom-call | flops 402653184 | bytes 3145728 | tf_op jit(solution)/shard_map/pallas_call | solution.py:373
  21.1 0.7 %collective-permute-start.6 = (f32[1,512,128]{2,1,0:T(8,128)S(1)}, f32[1,512,128]{2,1,0:T(8,128)S(1)}, u32[]{:S(2)}, u32[]{:S(2)}) collective-permute-start(f32[1,512,128]{2,1,0:T(8,128)S(1)} %shard_map.63), channel_id=1, source_target_pairs={{0,2},{1,3},{2,0},{3,1},{4,6},{5,7},{6,4},{7,5},{8,10},{9,11},{10,... | collective-permute-start | bytes 786440 | tf_op jit(solution)/shard_map/ppermute | solution.py:411
  21.7 0.8 %shard_map.62 = (f32[1,512,128]{2,1,0:T(8,128)S(1)}, f32[1,512,128]{2,1,0:T(8,128)S(1)}) custom-call(f32[3,2,2,8,128]{4,3,2,1,0:T(8,128)S(1)} %get-tuple-element.28.coef, bf16[2,2,128,512]{3,2,1,0:T(8,128)(2,1)S(1)} %get-tuple-element.43.refs_0_, bf16[2,3,256,256]{3,2,1,0:T(8,128)(2,1)S(1)} %shard_map.59.refs_1_, f32[2,512,128]{2,1,0:T(8,128)S(1)} %shard_map.57.refs_2_, ...), custom_call_target="tpu_custom_call" | custom-call | flops 402653184 | bytes 3457024 | tf_op jit(solution)/shard_map/pallas_call | solution.py:373
  22.5 0.8 %shard_map.64 = (f32[1,512,128]{2,1,0:T(8,128)S(1)}, f32[1,512,128]{2,1,0:T(8,128)S(1)}) custom-call(f32[3,2,2,8,128]{4,3,2,1,0:T(8,128)S(1)} %get-tuple-element.28.coef, bf16[2,2,128,512]{3,2,1,0:T(8,128)(2,1)S(1)} %get-tuple-element.43.refs_0_, bf16[2,3,256,256]{3,2,1,0:T(8,128)(2,1)S(1)} %shard_map.59.refs_1_, f32[2,512,128]{2,1,0:T(8,128)S(1)} %shard_map.57.refs_2_, ...), custom_call_target="tpu_custom_call" | custom-call | flops 402653184 | bytes 3457024 | tf_op jit(solution)/shard_map/pallas_call | solution.py:373
  23.3 4.7 %collective-permute-done.3.back = f32[1,512,128]{2,1,0:T(8,128)S(1)} collective-permute-done((f32[1,512,128]{2,1,0:T(8,128)S(1)}, f32[1,512,128]{2,1,0:T(8,128)S(1)}, u32[]{:S(2)}, u32[]{:S(2)}) %collective-permute-start.3) | collective-permute-done | bytes 262176 | tf_op jit(solution)/shard_map/ppermute | solution.py:411
  28.0 0.8 %shard_map.65.refs_0_ = f32[2,2,512,128]{3,2,1,0:T(8,128)} custom-call(f32[1,512,128]{2,1,0:T(8,128)S(1)} %get-tuple-element.44.part0, f32[1,512,128]{2,1,0:T(8,128)S(1)} %get-tuple-element.45.part1, f32[1,512,128]{2,1,0:T(8,128)S(1)} %collective-permute-done.3.back, f32[3,2,2,8,128]{4,3,2,1,0:T(8,128)S(1)} %get-tuple-element.28.coef), custom_call_target="tpu_custom_call" | custom-call | bytes 1835008 | tf_op jit(solution)/shard_map/pallas_call | solution.py:387
  28.9 4.3 %collective-permute-done.6.back = f32[1,512,128]{2,1,0:T(8,128)S(1)} collective-permute-done((f32[1,512,128]{2,1,0:T(8,128)S(1)}, f32[1,512,128]{2,1,0:T(8,128)S(1)}, u32[]{:S(2)}, u32[]{:S(2)}) %collective-permute-start.6) | collective-permute-done | bytes 262176 | tf_op jit(solution)/shard_map/ppermute | solution.py:411
  33.2 0.8 %shard_map.66 = f32[2,2,512,128]{3,2,1,0:T(8,128)} custom-call(f32[1,512,128]{2,1,0:T(8,128)S(1)} %get-tuple-element.41.part0, f32[1,512,128]{2,1,0:T(8,128)S(1)} %get-tuple-element.42.part1, f32[1,512,128]{2,1,0:T(8,128)S(1)} %collective-permute-done.6.back, f32[3,2,2,8,128]{4,3,2,1,0:T(8,128)S(1)} %get-tuple-element.28.coef, ...), custom_call_target="tpu_custom_call", output_to_operand_aliasing={{}: (4, {})} | custom-call | bytes 1835008 | tf_op jit(solution)/shard_map/pallas_call | solution.py:387
Async XLA Ops:
  1.1 6.0 %copy-start = (f32[2,131072]{1,0:T(2,128)S(1)}, f32[2,131072]{1,0:T(2,128)}, u32[]{:S(2)}) copy-start(f32[2,131072]{1,0:T(2,128)} %param.5) | copy-start | bytes 3145732
  1.1 9.7 %collective-permute-start = (f32[1,512,128]{2,1,0:T(8,128)S(1)}, f32[1,512,128]{2,1,0:T(8,128)S(1)}, u32[]{:S(2)}, u32[]{:S(2)}) collective-permute-start(f32[1,512,128]{2,1,0:T(8,128)S(1)} %get-tuple-element.48), channel_id=1, source_target_pairs={{0,2},{1,3},{2,0},{3,1},{4,6},{5,7},{6,4},{7,5},{8,10},{9,11},{10,... | collective-permute-start | bytes 786440 | tf_op jit(solution)/shard_map/ppermute | solution.py:411
  7.6 10.4 %collective-permute-start.1 = (f32[2,512,128]{2,1,0:T(8,128)S(1)}, f32[2,512,128]{2,1,0:T(8,128)S(1)}, u32[]{:S(2)}, u32[]{:S(2)}) collective-permute-start(f32[2,512,128]{2,1,0:T(8,128)S(1)} %shard_map.57.refs_2_), channel_id=1, source_target_pairs={{0,1},{1,0},{2,3},{3,2},{4,5},{5,4},{6,7},{7,6},{8,9},{9,8},{10,11... | collective-permute-start | bytes 1572872 | tf_op jit(solution)/shard_map/ppermute | solution.py:411
  7.7 8.7 %collective-permute-start.4 = (f32[1,512,128]{2,1,0:T(8,128)S(1)}, f32[1,512,128]{2,1,0:T(8,128)S(1)}, u32[]{:S(2)}, u32[]{:S(2)}) collective-permute-start(f32[1,512,128]{2,1,0:T(8,128)S(1)} %get-tuple-element.47), channel_id=1, source_target_pairs={{0,2},{1,3},{2,0},{3,1},{4,6},{5,7},{6,4},{7,5},{8,10},{9,11},{10,... | collective-permute-start | bytes 786440 | tf_op jit(solution)/shard_map/ppermute | solution.py:411
  11.2 6.8 %collective-permute-start.2 = (f32[1,512,128]{2,1,0:T(8,128)S(1)}, f32[1,512,128]{2,1,0:T(8,128)S(1)}, u32[]{:S(2)}, u32[]{:S(2)}) collective-permute-start(f32[1,512,128]{2,1,0:T(8,128)S(1)} %shard_map.58.refs_4_), channel_id=1, source_target_pairs={{0,1},{1,0},{2,3},{3,2},{4,5},{5,4},{6,7},{7,6},{8,9},{9,8},{10,11... | collective-permute-start | bytes 786440 | tf_op jit(solution)/shard_map/ppermute | solution.py:411
  16.7 3.5 %collective-permute-start.5 = (f32[1,512,128]{2,1,0:T(8,128)S(1)}, f32[1,512,128]{2,1,0:T(8,128)S(1)}, u32[]{:S(2)}, u32[]{:S(2)}) collective-permute-start(f32[1,512,128]{2,1,0:T(8,128)S(1)} %shard_map.61.refs_4_), channel_id=1, source_target_pairs={{0,1},{1,0},{2,3},{3,2},{4,5},{5,4},{6,7},{7,6},{8,9},{9,8},{10,11... | collective-permute-start | bytes 786440 | tf_op jit(solution)/shard_map/ppermute | solution.py:411
  18.8 9.2 %collective-permute-start.3 = (f32[1,512,128]{2,1,0:T(8,128)S(1)}, f32[1,512,128]{2,1,0:T(8,128)S(1)}, u32[]{:S(2)}, u32[]{:S(2)}) collective-permute-start(f32[1,512,128]{2,1,0:T(8,128)S(1)} %shard_map.60), channel_id=1, source_target_pairs={{0,2},{1,3},{2,0},{3,1},{4,6},{5,7},{6,4},{7,5},{8,10},{9,11},{10,... | collective-permute-start | bytes 786440 | tf_op jit(solution)/shard_map/ppermute | solution.py:411
  21.1 12.1 %collective-permute-start.6 = (f32[1,512,128]{2,1,0:T(8,128)S(1)}, f32[1,512,128]{2,1,0:T(8,128)S(1)}, u32[]{:S(2)}, u32[]{:S(2)}) collective-permute-start(f32[1,512,128]{2,1,0:T(8,128)S(1)} %shard_map.63), channel_id=1, source_target_pairs={{0,2},{1,3},{2,0},{3,1},{4,6},{5,7},{6,4},{7,5},{8,10},{9,11},{10,... | collective-permute-start | bytes 786440 | tf_op jit(solution)/shard_map/ppermute | solution.py:411

commit v3 on v2

--- a/solution.py
+++ b/solution.py
@@ -248,13 +248,18 @@
     return gate
 
 
-def second_kernel(units, flags, coef, w1_ref, re_ref, im_ref, m_re, m_im):
+def second_kernel(units, flags, re, im):
+    gdim = units.shape[-1]
+    h0, h1 = my_bits()
+    compose(units.shape[0] // 2, h1 * gdim + h0 * (gdim // 2), chosen(units, flags), (re, im))
+
+
+def half_kernel(units, flags, coef, m_re, m_im, w1_ref, re_ref, im_ref):
     count = units.shape[0] // 2
     gdim = units.shape[-1]
     half = gdim // 2
-    h0, h1 = my_bits()
+    _, h1 = my_bits()
     gate = chosen(units, flags)
-    compose(count, h1 * gdim + h0 * half, gate, (m_re, m_im))
     for k in range(2):
         at = lax.rem(h1 + k, 2) * gdim
         r, i = 0.0, 0.0
@@ -439,17 +444,18 @@
         + [dma((3,)), dma((ngates,)), dma((2 * count,))],
         flops=count * step,
     )
-    w1, re2, im2 = call(
-        second_kernel,
-        [bf16((2, 2, half, rows)), m, m],
-        [units, flags, coef],
-        [VM] * 3,
-        [m_scratch, m_scratch],
-        flops=3 * count * step // 2,
-    )
+    re1, im1 = call(second_kernel, [m, m], [units, flags], [VM] * 2, flops=count * step)
+    w0, re1 = tie((w0, re1))
     (kept,) = call(kept_kernel, [both], [w0, view], [VM] * 2, flops=2 * enter_flops)
     kept_other = other(kept, 1)
-    re2, kept = tie((re2, kept))
+    units, kept = tie((units, kept))
+    w1, re2, im2 = call(
+        half_kernel,
+        [bf16((2, 2, half, rows)), m, m],
+        [units, flags, coef, re1, im1],
+        [VM] * 5,
+        flops=count * step // 2,
+    )
     came[0], re2 = tie((came[0], re2))
     (mine,) = call(came_kernel, [block], [w0, came[0]], [VM] * 2, flops=enter_flops)
     re2, mine = tie((re2, mine))

time: 34.2 us -> 35.9 us (1.050)
  waiting for transfers between devices: 14.6 us -> 15.8 us
    ppermute x7, waiting for transfers between devices: 14.6 us -> 15.8 us  [other(): return lax.ppermute(v, 'qa', [(i, i ^ bit) for i in range(devices)])]
    pallas_call x10 -> x11, Pallas kernels: 10.9 us -> 11.2 us  [call(): pl.pallas_call(body, out_shape=outs, in_specs=specs, out_specs=[VM] * len...]
  transfers between devices with their start and end apart: 7 -> 7, of which waited for: 4 -> 3; matrix products, arithmetic and copies ran while one was open for 0% -> 0% of each run, Pallas kernels for 35% -> 34%
where the time goes in v3:
time: 35.9 us; the launch traced here: 35.7 us
  waiting for transfers between devices  15.8 us (44%)
  Pallas kernels  12.8 us (36%)
  starting transfers between devices  5.9 us (16%)
  local copies, waits for them, and re-layouts  1.07 us (3%)
    ppermute x7, waiting for transfers between devices, other(): return lax.ppermute(v, 'qa', [(i, i ^ bit) for i in range(devices)])  15.8 us
    pallas_call x11, Pallas kernels, call(): pl.pallas_call(body, out_shape=outs, in_specs=specs, out_specs=[VM] * len...  11.2 us
    ppermute x7, starting transfers between devices, other(): return lax.ppermute(v, 'qa', [(i, i ^ bit) for i in range(devices)])  5.9 us
    pallas_call x2, Pallas kernels, finish(): pl.pallas_call(partial(last_kernel, chunk), out_shape=shape, in_specs=[VM...  1.68 us
    dynamic_slice x1, local copies, waits for them, and re-layouts, block_of(): return lax.dynamic_slice_in_dim(v, (1 - h1) * 2 + c, 1, axis=0)  1.06 us
  transfers between devices with their start and end apart: 7, of which 3 were waited for; matrix products, arithmetic and copies ran while one was open for 0% of the time, Pallas kernels for 34%

profile of v3, /device:TPU:0, one launch (start us, length us, event | category | flops | bytes accessed | tf_op | source)
XLA Modules:
  0.0 35.7 jit_solution(5059195164795975344)
XLA Ops:
  0.0 1.1 %constant_dynamic-slice_fusion = (f32[1,512,128]{2,1,0:T(8,128)S(1)}, f32[1,512,128]{2,1,0:T(8,128)S(1)}) fusion(f32[4,512,128]{2,1,0:T(8,128)} %bitcast.10, s32[]{:T(128)S(6)} %select_n.7, s32[]{:T(128)S(6)} %select_n.6), kind=kLoop, calls=%fused_computation | loop fusion | bytes 1048584 | tf_op jit(solution)/shard_map/dynamic_slice | solution.py:419
  1.1 3.0 %collective-permute-start = (f32[1,512,128]{2,1,0:T(8,128)S(1)}, f32[1,512,128]{2,1,0:T(8,128)S(1)}, u32[]{:S(2)}, u32[]{:S(2)}) collective-permute-start(f32[1,512,128]{2,1,0:T(8,128)S(1)} %get-tuple-element.56), channel_id=1, source_target_pairs={{0,2},{1,3},{2,0},{3,1},{4,6},{5,7},{6,4},{7,5},{8,10},{9,11},{10,... | collective-permute-start | bytes 786440 | tf_op jit(solution)/shard_map/ppermute | solution.py:416
  4.1 2.9 %shard_map.55 = (bf16[2,3,256,256]{3,2,1,0:T(8,128)(2,1)S(1)}, f32[8,2,128,128]{3,2,1,0:T(8,128)S(1)}, s32[8,128]{1,0:T(8,128)S(1)}, f32[3,2,2,8,128]{4,3,2,1,0:T(8,128)S(1)}) custom-call(s32[12]{0:T(128)} %order.1, s32[12]{0:T(128)} %starts.1, f32[2,2,2,2]{3,2,1,0:T(2,128)} %pair.1, f32[12,2,128,128]{3,2,1,0:T(8,128)} %unit.1), custom_call_target="tpu_custom_call" | custom-call | flops 805306368 | bytes 3461280 | tf_op jit(solution)/shard_map/pallas_call | solution.py:378
  7.0 0.0 copy-start
  7.1 1.7 %shard_map.56 = (f32[2,256,128]{2,1,0:T(8,128)S(1)}, f32[2,256,128]{2,1,0:T(8,128)S(1)}) custom-call(f32[8,2,128,128]{3,2,1,0:T(8,128)S(1)} %get-tuple-element.35.units, s32[8,128]{1,0:T(8,128)S(1)} %get-tuple-element.32.flags), custom_call_target="tpu_custom_call" | custom-call | flops 805306368 | bytes 1576960 | tf_op jit(solution)/shard_map/pallas_call | solution.py:378
  8.8 0.0 copy-done
  8.8 0.5 %shard_map.57.refs_2_ = f32[2,512,128]{2,1,0:T(8,128)S(1)} custom-call(bf16[2,3,256,256]{3,2,1,0:T(8,128)(2,1)S(1)} %get-tuple-element.34.w_ref, f32[4,512,128]{2,1,0:T(8,128)S(1)} %bitcast.11), custom_call_target="tpu_custom_call" | custom-call | flops 402653184 | bytes 2359296 | tf_op jit(solution)/shard_map/pallas_call | solution.py:378
  9.3 0.1 collective-permute-start.1
  9.4 0.1 collective-permute-start.4
  9.5 1.0 %shard_map.58 = (bf16[2,2,128,512]{3,2,1,0:T(8,128)(2,1)S(1)}, f32[2,256,128]{2,1,0:T(8,128)S(1)}, f32[2,256,128]{2,1,0:T(8,128)S(1)}) custom-call(f32[8,2,128,128]{3,2,1,0:T(8,128)S(1)} %get-tuple-element.35.units, s32[8,128]{1,0:T(8,128)S(1)} %get-tuple-element.32.flags, f32[3,2,2,8,128]{4,3,2,1,0:T(8,128)S(1)} %get-tuple-element.36.coef, ...), custom_call_target="tpu_custom_call" | custom-call | flops 402653184 | bytes 2674688 | tf_op jit(solution)/shard_map/pallas_call | solution.py:378
  10.5 0.0 collective-permute-done.raw
  10.5 0.4 %shard_map.59.refs_4_ = f32[1,512,128]{2,1,0:T(8,128)S(1)} custom-call(bf16[2,3,256,256]{3,2,1,0:T(8,128)(2,1)S(1)} %get-tuple-element.34.w_ref, f32[1,512,128]{2,1,0:T(8,128)S(1)} %collective-permute-done.raw), custom_call_target="tpu_custom_call" | custom-call | flops 201326592 | bytes 1310720 | tf_op jit(solution)/shard_map/pallas_call | solution.py:378
  10.9 0.5 %collective-permute-start.2 = (f32[1,512,128]{2,1,0:T(8,128)S(1)}, f32[1,512,128]{2,1,0:T(8,128)S(1)}, u32[]{:S(2)}, u32[]{:S(2)}) collective-permute-start(f32[1,512,128]{2,1,0:T(8,128)S(1)} %shard_map.59.refs_4_), channel_id=1, source_target_pairs={{0,1},{1,0},{2,3},{3,2},{4,5},{5,4},{6,7},{7,6},{8,9},{9,8},{10,11... | collective-permute-start | bytes 786440 | tf_op jit(solution)/shard_map/ppermute | solution.py:416
  11.3 6.7 %collective-permute-done.4.raw = f32[1,512,128]{2,1,0:T(8,128)S(1)} collective-permute-done((f32[1,512,128]{2,1,0:T(8,128)S(1)}, f32[1,512,128]{2,1,0:T(8,128)S(1)}, u32[]{:S(2)}, u32[]{:S(2)}) %collective-permute-start.4) | collective-permute-done | bytes 262176 | tf_op jit(solution)/shard_map/ppermute | solution.py:416
  18.1 0.4 %shard_map.62.refs_4_ = f32[1,512,128]{2,1,0:T(8,128)S(1)} custom-call(bf16[2,3,256,256]{3,2,1,0:T(8,128)(2,1)S(1)} %get-tuple-element.34.w_ref, f32[1,512,128]{2,1,0:T(8,128)S(1)} %collective-permute-done.4.raw), custom_call_target="tpu_custom_call" | custom-call | flops 201326592 | bytes 1310720 | tf_op jit(solution)/shard_map/pallas_call | solution.py:378
  18.5 0.1 collective-permute-start.5
  18.6 1.1 %shard_map.60.refs_1_ = bf16[2,3,256,256]{3,2,1,0:T(8,128)(2,1)S(1)} custom-call(f32[8,2,128,128]{3,2,1,0:T(8,128)S(1)} %get-tuple-element.35.units, s32[8,128]{1,0:T(8,128)S(1)} %get-tuple-element.32.flags, f32[2,256,128]{2,1,0:T(8,128)S(1)} %get-tuple-element.43.re, f32[2,256,128]{2,1,0:T(8,128)S(1)} %get-tuple-element.44.im), custom_call_target="tpu_custom_call" | custom-call | flops 402653184 | bytes 2363392 | tf_op jit(solution)/shard_map/pallas_call | solution.py:378
  19.7 0.0 collective-permute-done.2.refs_5_
  19.7 0.0 collective-permute-done.1.refs_3_
  19.7 0.8 %shard_map.61 = f32[1,512,128]{2,1,0:T(8,128)S(1)} custom-call(bf16[2,2,128,512]{3,2,1,0:T(8,128)(2,1)S(1)} %get-tuple-element.51.refs_0_, bf16[2,3,256,256]{3,2,1,0:T(8,128)(2,1)S(1)} %shard_map.60.refs_1_, f32[2,512,128]{2,1,0:T(8,128)S(1)} %shard_map.57.refs_2_, f32[2,512,128]{2,1,0:T(8,128)S(1)} %collective-permute-done.1.refs_3_, ...), custom_call_target="tpu_custom_call" | custom-call | flops 402653184 | bytes 3145728 | tf_op jit(solution)/shard_map/pallas_call | solution.py:378
  20.5 0.4 collective-permute-start.3
  20.9 0.0 collective-permute-done.5.refs_5_
  20.9 0.8 %shard_map.64 = f32[1,512,128]{2,1,0:T(8,128)S(1)} custom-call(bf16[2,2,128,512]{3,2,1,0:T(8,128)(2,1)S(1)} %get-tuple-element.51.refs_0_, bf16[2,3,256,256]{3,2,1,0:T(8,128)(2,1)S(1)} %shard_map.60.refs_1_, f32[2,512,128]{2,1,0:T(8,128)S(1)} %shard_map.57.refs_2_, f32[2,512,128]{2,1,0:T(8,128)S(1)} %collective-permute-done.1.refs_3_, ...), custom_call_target="tpu_custom_call" | custom-call | flops 402653184 | bytes 3145728 | tf_op jit(solution)/shard_map/pallas_call | solution.py:378
  21.6 1.8 %collective-permute-start.6 = (f32[1,512,128]{2,1,0:T(8,128)S(1)}, f32[1,512,128]{2,1,0:T(8,128)S(1)}, u32[]{:S(2)}, u32[]{:S(2)}) collective-permute-start(f32[1,512,128]{2,1,0:T(8,128)S(1)} %shard_map.64), channel_id=1, source_target_pairs={{0,2},{1,3},{2,0},{3,1},{4,6},{5,7},{6,4},{7,5},{8,10},{9,11},{10,... | collective-permute-start | bytes 786440 | tf_op jit(solution)/shard_map/ppermute | solution.py:416
  23.4 0.8 %shard_map.63 = (f32[1,512,128]{2,1,0:T(8,128)S(1)}, f32[1,512,128]{2,1,0:T(8,128)S(1)}) custom-call(f32[3,2,2,8,128]{4,3,2,1,0:T(8,128)S(1)} %get-tuple-element.36.coef, bf16[2,2,128,512]{3,2,1,0:T(8,128)(2,1)S(1)} %get-tuple-element.51.refs_0_, bf16[2,3,256,256]{3,2,1,0:T(8,128)(2,1)S(1)} %shard_map.60.refs_1_, f32[2,512,128]{2,1,0:T(8,128)S(1)} %shard_map.57.refs_2_, ...), custom_call_target="tpu_custom_call" | custom-call | flops 402653184 | bytes 3457024 | tf_op jit(solution)/shard_map/pallas_call | solution.py:378
  24.2 0.8 %shard_map.65 = (f32[1,512,128]{2,1,0:T(8,128)S(1)}, f32[1,512,128]{2,1,0:T(8,128)S(1)}) custom-call(f32[3,2,2,8,128]{4,3,2,1,0:T(8,128)S(1)} %get-tuple-element.36.coef, bf16[2,2,128,512]{3,2,1,0:T(8,128)(2,1)S(1)} %get-tuple-element.51.refs_0_, bf16[2,3,256,256]{3,2,1,0:T(8,128)(2,1)S(1)} %shard_map.60.refs_1_, f32[2,512,128]{2,1,0:T(8,128)S(1)} %shard_map.57.refs_2_, ...), custom_call_target="tpu_custom_call" | custom-call | flops 402653184 | bytes 3457024 | tf_op jit(solution)/shard_map/pallas_call | solution.py:378
  25.0 4.7 %collective-permute-done.3.back = f32[1,512,128]{2,1,0:T(8,128)S(1)} collective-permute-done((f32[1,512,128]{2,1,0:T(8,128)S(1)}, f32[1,512,128]{2,1,0:T(8,128)S(1)}, u32[]{:S(2)}, u32[]{:S(2)}) %collective-permute-start.3) | collective-permute-done | bytes 262176 | tf_op jit(solution)/shard_map/ppermute | solution.py:416
  29.7 0.8 %shard_map.66.refs_0_ = f32[2,2,512,128]{3,2,1,0:T(8,128)} custom-call(f32[1,512,128]{2,1,0:T(8,128)S(1)} %get-tuple-element.52.part0, f32[1,512,128]{2,1,0:T(8,128)S(1)} %get-tuple-element.53.part1, f32[1,512,128]{2,1,0:T(8,128)S(1)} %collective-permute-done.3.back, f32[3,2,2,8,128]{4,3,2,1,0:T(8,128)S(1)} %get-tuple-element.36.coef), custom_call_target="tpu_custom_call" | custom-call | bytes 1835008 | tf_op jit(solution)/shard_map/pallas_call | solution.py:392
  30.6 4.3 %collective-permute-done.6.back = f32[1,512,128]{2,1,0:T(8,128)S(1)} collective-permute-done((f32[1,512,128]{2,1,0:T(8,128)S(1)}, f32[1,512,128]{2,1,0:T(8,128)S(1)}, u32[]{:S(2)}, u32[]{:S(2)}) %collective-permute-start.6) | collective-permute-done | bytes 262176 | tf_op jit(solution)/shard_map/ppermute | solution.py:416
  34.9 0.8 %shard_map.67 = f32[2,2,512,128]{3,2,1,0:T(8,128)} custom-call(f32[1,512,128]{2,1,0:T(8,128)S(1)} %get-tuple-element.49.part0, f32[1,512,128]{2,1,0:T(8,128)S(1)} %get-tuple-element.50.part1, f32[1,512,128]{2,1,0:T(8,128)S(1)} %collective-permute-done.6.back, f32[3,2,2,8,128]{4,3,2,1,0:T(8,128)S(1)} %get-tuple-element.36.coef, ...), custom_call_target="tpu_custom_call", output_to_operand_aliasing={{}: (4, {})} | custom-call | bytes 1835008 | tf_op jit(solution)/shard_map/pallas_call | solution.py:392
Async XLA Ops:
  1.1 9.4 %collective-permute-start = (f32[1,512,128]{2,1,0:T(8,128)S(1)}, f32[1,512,128]{2,1,0:T(8,128)S(1)}, u32[]{:S(2)}, u32[]{:S(2)}) collective-permute-start(f32[1,512,128]{2,1,0:T(8,128)S(1)} %get-tuple-element.56), channel_id=1, source_target_pairs={{0,2},{1,3},{2,0},{3,1},{4,6},{5,7},{6,4},{7,5},{8,10},{9,11},{10,... | collective-permute-start | bytes 786440 | tf_op jit(solution)/shard_map/ppermute | solution.py:416
  7.0 1.7 %copy-start = (f32[2,131072]{1,0:T(2,128)S(1)}, f32[2,131072]{1,0:T(2,128)}, u32[]{:S(2)}) copy-start(f32[2,131072]{1,0:T(2,128)} %param.5) | copy-start | bytes 3145732
  9.3 10.4 %collective-permute-start.1 = (f32[2,512,128]{2,1,0:T(8,128)S(1)}, f32[2,512,128]{2,1,0:T(8,128)S(1)}, u32[]{:S(2)}, u32[]{:S(2)}) collective-permute-start(f32[2,512,128]{2,1,0:T(8,128)S(1)} %shard_map.57.refs_2_), channel_id=1, source_target_pairs={{0,1},{1,0},{2,3},{3,2},{4,5},{5,4},{6,7},{7,6},{8,9},{9,8},{10,11... | collective-permute-start | bytes 1572872 | tf_op jit(solution)/shard_map/ppermute | solution.py:416
  9.4 8.7 %collective-permute-start.4 = (f32[1,512,128]{2,1,0:T(8,128)S(1)}, f32[1,512,128]{2,1,0:T(8,128)S(1)}, u32[]{:S(2)}, u32[]{:S(2)}) collective-permute-start(f32[1,512,128]{2,1,0:T(8,128)S(1)} %get-tuple-element.55), channel_id=1, source_target_pairs={{0,2},{1,3},{2,0},{3,1},{4,6},{5,7},{6,4},{7,5},{8,10},{9,11},{10,... | collective-permute-start | bytes 786440 | tf_op jit(solution)/shard_map/ppermute | solution.py:416
  10.9 8.8 %collective-permute-start.2 = (f32[1,512,128]{2,1,0:T(8,128)S(1)}, f32[1,512,128]{2,1,0:T(8,128)S(1)}, u32[]{:S(2)}, u32[]{:S(2)}) collective-permute-start(f32[1,512,128]{2,1,0:T(8,128)S(1)} %shard_map.59.refs_4_), channel_id=1, source_target_pairs={{0,1},{1,0},{2,3},{3,2},{4,5},{5,4},{6,7},{7,6},{8,9},{9,8},{10,11... | collective-permute-start | bytes 786440 | tf_op jit(solution)/shard_map/ppermute | solution.py:416
  18.5 2.4 %collective-permute-start.5 = (f32[1,512,128]{2,1,0:T(8,128)S(1)}, f32[1,512,128]{2,1,0:T(8,128)S(1)}, u32[]{:S(2)}, u32[]{:S(2)}) collective-permute-start(f32[1,512,128]{2,1,0:T(8,128)S(1)} %shard_map.62.refs_4_), channel_id=1, source_target_pairs={{0,1},{1,0},{2,3},{3,2},{4,5},{5,4},{6,7},{7,6},{8,9},{9,8},{10,11... | collective-permute-start | bytes 786440 | tf_op jit(solution)/shard_map/ppermute | solution.py:416
  20.5 9.2 %collective-permute-start.3 = (f32[1,512,128]{2,1,0:T(8,128)S(1)}, f32[1,512,128]{2,1,0:T(8,128)S(1)}, u32[]{:S(2)}, u32[]{:S(2)}) collective-permute-start(f32[1,512,128]{2,1,0:T(8,128)S(1)} %shard_map.61), channel_id=1, source_target_pairs={{0,2},{1,3},{2,0},{3,1},{4,6},{5,7},{6,4},{7,5},{8,10},{9,11},{10,... | collective-permute-start | bytes 786440 | tf_op jit(solution)/shard_map/ppermute | solution.py:416
  21.6 13.3 %collective-permute-start.6 = (f32[1,512,128]{2,1,0:T(8,128)S(1)}, f32[1,512,128]{2,1,0:T(8,128)S(1)}, u32[]{:S(2)}, u32[]{:S(2)}) collective-permute-start(f32[1,512,128]{2,1,0:T(8,128)S(1)} %shard_map.64), channel_id=1, source_target_pairs={{0,2},{1,3},{2,0},{3,1},{4,6},{5,7},{6,4},{7,5},{8,10},{9,11},{10,... | collective-permute-start | bytes 786440 | tf_op jit(solution)/shard_map/ppermute | solution.py:416

commit v4 on v2

--- a/solution.py
+++ b/solution.py
@@ -194,10 +194,10 @@
     return ref[at, pl.ds(0, rows, stride=2), :], ref[at, pl.ds(1, rows, stride=2), :]
 
 
-def front_kernel(order, starts, pair, unit, w0_ref, units, flags, coef, *scratch):
+def front_kernel(order, starts, pair, unit, w0_ref, w1_ref, units, flags, coef, *scratch):
     order_s, starts_s, pair_s, u, m_re, m_im, small_sems, sems, late_sems = scratch
-    ngates, later = unit.shape[0], units.shape[0]
-    count = ngates - later
+    ngates, later, gdim = unit.shape[0], units.shape[0], unit.shape[-1]
+    count, half = ngates - later, gdim // 2
     h0, h1 = my_bits()
     smalls = [
         pltpu.make_async_copy(a, b, small_sems.at[i])
@@ -224,15 +224,28 @@
         fetch(g).wait()
         return u[g, 0], u[g, 1], starts_s[i]
 
-    compose(count, 0, gate, (m_re, m_im))
+    compose(later, 0, gate, (m_re, m_im))
     put(w0_ref, whole(m_re), whole(m_im))
+    compose(later, h1 * gdim + h0 * half, lambda i: gate(later + i), (m_re, m_im))
+    for k in range(2):
+        at = lax.rem(h1 + k, 2) * gdim
+        r, i = 0.0, 0.0
+        for b in range(2):
+            rows = pl.ds(pl.multiple_of(at + b * half, half), half)
+            v_re, v_im = pair_s[1, 0, h0, b], pair_s[1, 1, h0, b]
+            x_re, x_im = (
+                jnp.concatenate([m[j, rows, :] for j in range(2)], axis=1) for m in (m_re, m_im)
+            )
+            r += v_re * x_re - v_im * x_im
+            i += v_re * x_im + v_im * x_re
+        w1_ref[0, k], w1_ref[1, k] = split(embed(r, i))
     bits = starts_s[count]
     for k in range(1, later):
         bits += starts_s[count + k] * 2**k
     flags[...] = jnp.full(flags.shape, bits, jnp.int32)
     for b in range(2):
         for p in range(2):
-            for i, v in enumerate((pair_s[0, p, b, h1], pair_s[0, p, b, 1 - h1], pair_s[1, p, h0, b])):
+            for i, v in enumerate((pair_s[0, p, b, h1], pair_s[0, p, b, 1 - h1])):
                 coef[i, b, p] = jnp.full(coef.shape[3:], v, F32)
     for k in range(later):
         fetch(order_s[count + k]).wait()
@@ -248,33 +261,15 @@
     return gate
 
 
-def second_kernel(units, flags, coef, w1_ref, re_ref, im_ref, m_re, m_im):
-    count = units.shape[0] // 2
-    gdim = units.shape[-1]
-    half = gdim // 2
-    h0, h1 = my_bits()
-    gate = chosen(units, flags)
-    compose(count, h1 * gdim + h0 * half, gate, (m_re, m_im))
-    for k in range(2):
-        at = lax.rem(h1 + k, 2) * gdim
-        r, i = 0.0, 0.0
-        for b in range(2):
-            rows = pl.ds(pl.multiple_of(at + b * half, half), half)
-            v_re, v_im = coef[2, b, 0][:1, :1], coef[2, b, 1][:1, :1]
-            x_re, x_im = (
-                jnp.concatenate([m[j, rows, :] for j in range(2)], axis=1) for m in (m_re, m_im)
-            )
-            r += v_re * x_re - v_im * x_im
-            i += v_re * x_im + v_im * x_re
-        w1_ref[0, k], w1_ref[1, k] = split(embed(r, i))
-    compose(count // 2, 0, lambda i: gate(count + i), (re_ref, im_ref))
+def half_kernel(units, flags, re, im):
+    compose(units.shape[0] // 2, 0, chosen(units, flags), (re, im))
 
 
 def third_kernel(units, flags, re, im, w_ref, m_re, m_im):
-    count = units.shape[0] // 2
+    count = units.shape[0]
     gate = chosen(units, flags)
     source = (re, im)
-    for k in range(count + count // 2, 2 * count):
+    for k in range(count // 2, count):
         apply(*gate(k), source, (m_re, m_im))
         source = (m_re, m_im)
     put(w_ref, whole(source[0]), whole(source[1]))
@@ -424,32 +419,26 @@
     ngates = unitaries.shape[0]
     tile = (8, lanes)
     dma = pltpu.SemaphoreType.DMA
-    w0, units, flags, coef = call(
+    w0, w1, units, flags, coef = call(
         front_kernel,
         [
             bf16((2, 3, dim, dim)),
-            f32((2 * count, *unitaries.shape[1:])),
+            bf16((2, 2, half, rows)),
+            f32((count, *unitaries.shape[1:])),
             jax.ShapeDtypeStruct(tile, jnp.int32),
-            f32((3, 2, 2, *tile)),
+            f32((2, 2, 2, *tile)),
         ],
         [far(v) for v in (*small, unitaries)],
         [HB] * 4,
         [pltpu.SMEM(v.shape, v.dtype) for v in small]
         + [pltpu.VMEM(unitaries.shape, F32), m_scratch, m_scratch]
-        + [dma((3,)), dma((ngates,)), dma((2 * count,))],
-        flops=count * step,
-    )
-    w1, re2, im2 = call(
-        second_kernel,
-        [bf16((2, 2, half, rows)), m, m],
-        [units, flags, coef],
-        [VM] * 3,
-        [m_scratch, m_scratch],
-        flops=3 * count * step // 2,
+        + [dma((3,)), dma((ngates,)), dma((count,))],
+        flops=2 * count * step,
     )
     (kept,) = call(kept_kernel, [both], [w0, view], [VM] * 2, flops=2 * enter_flops)
     kept_other = other(kept, 1)
-    re2, kept = tie((re2, kept))
+    units, kept = tie((units, kept))
+    re2, im2 = call(half_kernel, [m, m], [units, flags], [VM] * 2, flops=count * step // 2)
     came[0], re2 = tie((came[0], re2))
     (mine,) = call(came_kernel, [block], [w0, came[0]], [VM] * 2, flops=enter_flops)
     re2, mine = tie((re2, mine))

time: 34.2 us -> 35.7 us (1.044)
  waiting for transfers between devices: 14.6 us -> 16 us
    ppermute x7, waiting for transfers between devices: 14.6 us -> 16 us  [other(): return lax.ppermute(v, 'qa', [(i, i ^ bit) for i in range(devices)])]
  transfers between devices with their start and end apart: 7 -> 7, of which waited for: 4 -> 4; matrix products, arithmetic and copies ran while one was open for 0% -> 0% of each run, Pallas kernels for 35% -> 33%
where the time goes in v4:
time: 35.7 us; the launch traced here: 35.5 us
  waiting for transfers between devices  16 us (45%)
  Pallas kernels  12.5 us (35%)
  starting transfers between devices  5.75 us (16%)
  local copies, waits for them, and re-layouts  1.07 us (3%)
    ppermute x7, waiting for transfers between devices, other(): return lax.ppermute(v, 'qa', [(i, i ^ bit) for i in range(devices)])  16 us
    pallas_call x10, Pallas kernels, call(): pl.pallas_call(body, out_shape=outs, in_specs=specs, out_specs=[VM] * len...  10.8 us
    ppermute x7, starting transfers between devices, other(): return lax.ppermute(v, 'qa', [(i, i ^ bit) for i in range(devices)])  5.75 us
    pallas_call x2, Pallas kernels, finish(): pl.pallas_call(partial(last_kernel, chunk), out_shape=shape, in_specs=[VM...  1.68 us
    dynamic_slice x1, local copies, waits for them, and re-layouts, block_of(): return lax.dynamic_slice_in_dim(v, (1 - h1) * 2 + c, 1, axis=0)  1.06 us
  transfers between devices with their start and end apart: 7, of which 4 were waited for; matrix products, arithmetic and copies ran while one was open for 0% of the time, Pallas kernels for 33%

profile of v4, /device:TPU:0, one launch (start us, length us, event | category | flops | bytes accessed | tf_op | source)
XLA Modules:
  0.0 35.5 jit_solution(14528225904600217869)
XLA Ops:
  0.0 1.1 %constant_dynamic-slice_fusion = (f32[1,512,128]{2,1,0:T(8,128)S(1)}, f32[1,512,128]{2,1,0:T(8,128)S(1)}) fusion(f32[4,512,128]{2,1,0:T(8,128)} %bitcast.10, s32[]{:T(128)S(6)} %select_n.7, s32[]{:T(128)S(6)} %select_n.6), kind=kLoop, calls=%fused_computation | loop fusion | bytes 1048584 | tf_op jit(solution)/shard_map/dynamic_slice | solution.py:409
  1.1 0.0 copy-start
  1.1 3.0 %collective-permute-start = (f32[1,512,128]{2,1,0:T(8,128)S(1)}, f32[1,512,128]{2,1,0:T(8,128)S(1)}, u32[]{:S(2)}, u32[]{:S(2)}) collective-permute-start(f32[1,512,128]{2,1,0:T(8,128)S(1)} %get-tuple-element.48), channel_id=1, source_target_pairs={{0,2},{1,3},{2,0},{3,1},{4,6},{5,7},{6,4},{7,5},{8,10},{9,11},{10,... | collective-permute-start | bytes 786440 | tf_op jit(solution)/shard_map/ppermute | solution.py:406
  4.1 4.5 %shard_map.55 = (bf16[2,3,256,256]{3,2,1,0:T(8,128)(2,1)S(1)}, bf16[2,2,128,512]{3,2,1,0:T(8,128)(2,1)S(1)}, f32[4,2,128,128]{3,2,1,0:T(8,128)S(1)}, s32[8,128]{1,0:T(8,128)S(1)}, f32[2,2,2,8,128]{4,3,2,1,0:T(8,128)S(1)}) custom-call(s32[12]{0:T(128)} %order.1, s32[12]{0:T(128)} %starts.1, f32[2,2,2,2]{3,2,1,0:T(2,128)} %pair.1, f32[12,2,128,128]{3,2,1,0:T(8,128)} %unit.1), custom_call_target="tpu_custom_call" | custom-call | flops 1610612736 | bytes 3444896 | tf_op jit(solution)/shard_map/pallas_call | solution.py:368
  8.6 0.0 copy-done
  8.6 0.5 %shard_map.56.refs_2_ = f32[2,512,128]{2,1,0:T(8,128)S(1)} custom-call(bf16[2,3,256,256]{3,2,1,0:T(8,128)(2,1)S(1)} %get-tuple-element.28.w_ref, f32[4,512,128]{2,1,0:T(8,128)S(1)} %bitcast.11), custom_call_target="tpu_custom_call" | custom-call | flops 402653184 | bytes 2359296 | tf_op jit(solution)/shard_map/pallas_call | solution.py:368
  9.1 0.1 collective-permute-start.1
  9.2 0.2 collective-permute-start.4
  9.4 0.9 %shard_map.57 = (f32[2,256,128]{2,1,0:T(8,128)S(1)}, f32[2,256,128]{2,1,0:T(8,128)S(1)}) custom-call(f32[4,2,128,128]{3,2,1,0:T(8,128)S(1)} %get-tuple-element.29.units, s32[8,128]{1,0:T(8,128)S(1)} %get-tuple-element.30.flags), custom_call_target="tpu_custom_call" | custom-call | flops 402653184 | bytes 1052672 | tf_op jit(solution)/shard_map/pallas_call | solution.py:368
  10.2 0.2 collective-permute-done.raw
  10.4 0.4 %shard_map.58.refs_4_ = f32[1,512,128]{2,1,0:T(8,128)S(1)} custom-call(bf16[2,3,256,256]{3,2,1,0:T(8,128)(2,1)S(1)} %get-tuple-element.28.w_ref, f32[1,512,128]{2,1,0:T(8,128)S(1)} %collective-permute-done.raw), custom_call_target="tpu_custom_call" | custom-call | flops 201326592 | bytes 1310720 | tf_op jit(solution)/shard_map/pallas_call | solution.py:368
  10.8 0.3 collective-permute-start.2
  11.1 6.9 %collective-permute-done.4.raw = f32[1,512,128]{2,1,0:T(8,128)S(1)} collective-permute-done((f32[1,512,128]{2,1,0:T(8,128)S(1)}, f32[1,512,128]{2,1,0:T(8,128)S(1)}, u32[]{:S(2)}, u32[]{:S(2)}) %collective-permute-start.4) | collective-permute-done | bytes 262176 | tf_op jit(solution)/shard_map/ppermute | solution.py:406
  17.9 0.4 %shard_map.61.refs_4_ = f32[1,512,128]{2,1,0:T(8,128)S(1)} custom-call(bf16[2,3,256,256]{3,2,1,0:T(8,128)(2,1)S(1)} %get-tuple-element.28.w_ref, f32[1,512,128]{2,1,0:T(8,128)S(1)} %collective-permute-done.4.raw), custom_call_target="tpu_custom_call" | custom-call | flops 201326592 | bytes 1310720 | tf_op jit(solution)/shard_map/pallas_call | solution.py:368
  18.3 0.1 collective-permute-start.5
  18.4 1.1 %shard_map.59.refs_1_ = bf16[2,3,256,256]{3,2,1,0:T(8,128)(2,1)S(1)} custom-call(f32[4,2,128,128]{3,2,1,0:T(8,128)S(1)} %get-tuple-element.29.units, s32[8,128]{1,0:T(8,128)S(1)} %get-tuple-element.30.flags, f32[2,256,128]{2,1,0:T(8,128)S(1)} %get-tuple-element.34.re, f32[2,256,128]{2,1,0:T(8,128)S(1)} %get-tuple-element.35.im), custom_call_target="tpu_custom_call" | custom-call | flops 402653184 | bytes 1839104 | tf_op jit(solution)/shard_map/pallas_call | solution.py:368
  19.5 0.0 collective-permute-done.2.refs_5_
  19.5 0.0 collective-permute-done.1.refs_3_
  19.5 0.8 %shard_map.60 = f32[1,512,128]{2,1,0:T(8,128)S(1)} custom-call(bf16[2,2,128,512]{3,2,1,0:T(8,128)(2,1)S(1)} %get-tuple-element.43.refs_0_, bf16[2,3,256,256]{3,2,1,0:T(8,128)(2,1)S(1)} %shard_map.59.refs_1_, f32[2,512,128]{2,1,0:T(8,128)S(1)} %shard_map.56.refs_2_, f32[2,512,128]{2,1,0:T(8,128)S(1)} %collective-permute-done.1.refs_3_, ...), custom_call_target="tpu_custom_call" | custom-call | flops 402653184 | bytes 3145728 | tf_op jit(solution)/shard_map/pallas_call | solution.py:368
  20.3 0.3 collective-permute-start.3
  20.7 0.0 collective-permute-done.5.refs_5_
  20.7 0.8 %shard_map.63 = f32[1,512,128]{2,1,0:T(8,128)S(1)} custom-call(bf16[2,2,128,512]{3,2,1,0:T(8,128)(2,1)S(1)} %get-tuple-element.43.refs_0_, bf16[2,3,256,256]{3,2,1,0:T(8,128)(2,1)S(1)} %shard_map.59.refs_1_, f32[2,512,128]{2,1,0:T(8,128)S(1)} %shard_map.56.refs_2_, f32[2,512,128]{2,1,0:T(8,128)S(1)} %collective-permute-done.1.refs_3_, ...), custom_call_target="tpu_custom_call" | custom-call | flops 402653184 | bytes 3145728 | tf_op jit(solution)/shard_map/pallas_call | solution.py:368
  21.4 1.8 %collective-permute-start.6 = (f32[1,512,128]{2,1,0:T(8,128)S(1)}, f32[1,512,128]{2,1,0:T(8,128)S(1)}, u32[]{:S(2)}, u32[]{:S(2)}) collective-permute-start(f32[1,512,128]{2,1,0:T(8,128)S(1)} %shard_map.63), channel_id=1, source_target_pairs={{0,2},{1,3},{2,0},{3,1},{4,6},{5,7},{6,4},{7,5},{8,10},{9,11},{10,... | collective-permute-start | bytes 786440 | tf_op jit(solution)/shard_map/ppermute | solution.py:406
  23.2 0.8 %shard_map.62 = (f32[1,512,128]{2,1,0:T(8,128)S(1)}, f32[1,512,128]{2,1,0:T(8,128)S(1)}) custom-call(f32[2,2,2,8,128]{4,3,2,1,0:T(8,128)S(1)} %get-tuple-element.38.coef, bf16[2,2,128,512]{3,2,1,0:T(8,128)(2,1)S(1)} %get-tuple-element.43.refs_0_, bf16[2,3,256,256]{3,2,1,0:T(8,128)(2,1)S(1)} %shard_map.59.refs_1_, f32[2,512,128]{2,1,0:T(8,128)S(1)} %shard_map.56.refs_2_, ...), custom_call_target="tpu_custom_call" | custom-call | flops 402653184 | bytes 3440640 | tf_op jit(solution)/shard_map/pallas_call | solution.py:368
  24.0 0.8 %shard_map.64 = (f32[1,512,128]{2,1,0:T(8,128)S(1)}, f32[1,512,128]{2,1,0:T(8,128)S(1)}) custom-call(f32[2,2,2,8,128]{4,3,2,1,0:T(8,128)S(1)} %get-tuple-element.38.coef, bf16[2,2,128,512]{3,2,1,0:T(8,128)(2,1)S(1)} %get-tuple-element.43.refs_0_, bf16[2,3,256,256]{3,2,1,0:T(8,128)(2,1)S(1)} %shard_map.59.refs_1_, f32[2,512,128]{2,1,0:T(8,128)S(1)} %shard_map.56.refs_2_, ...), custom_call_target="tpu_custom_call" | custom-call | flops 402653184 | bytes 3440640 | tf_op jit(solution)/shard_map/pallas_call | solution.py:368
  24.8 4.7 %collective-permute-done.3.back = f32[1,512,128]{2,1,0:T(8,128)S(1)} collective-permute-done((f32[1,512,128]{2,1,0:T(8,128)S(1)}, f32[1,512,128]{2,1,0:T(8,128)S(1)}, u32[]{:S(2)}, u32[]{:S(2)}) %collective-permute-start.3) | collective-permute-done | bytes 262176 | tf_op jit(solution)/shard_map/ppermute | solution.py:406
  29.6 0.8 %shard_map.65.refs_0_ = f32[2,2,512,128]{3,2,1,0:T(8,128)} custom-call(f32[1,512,128]{2,1,0:T(8,128)S(1)} %get-tuple-element.44.part0, f32[1,512,128]{2,1,0:T(8,128)S(1)} %get-tuple-element.45.part1, f32[1,512,128]{2,1,0:T(8,128)S(1)} %collective-permute-done.3.back, f32[2,2,2,8,128]{4,3,2,1,0:T(8,128)S(1)} %get-tuple-element.38.coef), custom_call_target="tpu_custom_call" | custom-call | bytes 1835008 | tf_op jit(solution)/shard_map/pallas_call | solution.py:382
  30.4 4.3 %collective-permute-done.6.back = f32[1,512,128]{2,1,0:T(8,128)S(1)} collective-permute-done((f32[1,512,128]{2,1,0:T(8,128)S(1)}, f32[1,512,128]{2,1,0:T(8,128)S(1)}, u32[]{:S(2)}, u32[]{:S(2)}) %collective-permute-start.6) | collective-permute-done | bytes 262176 | tf_op jit(solution)/shard_map/ppermute | solution.py:406
  34.7 0.8 %shard_map.66 = f32[2,2,512,128]{3,2,1,0:T(8,128)} custom-call(f32[1,512,128]{2,1,0:T(8,128)S(1)} %get-tuple-element.41.part0, f32[1,512,128]{2,1,0:T(8,128)S(1)} %get-tuple-element.42.part1, f32[1,512,128]{2,1,0:T(8,128)S(1)} %collective-permute-done.6.back, f32[2,2,2,8,128]{4,3,2,1,0:T(8,128)S(1)} %get-tuple-element.38.coef, ...), custom_call_target="tpu_custom_call", output_to_operand_aliasing={{}: (4, {})} | custom-call | bytes 1835008 | tf_op jit(solution)/shard_map/pallas_call | solution.py:382
Async XLA Ops:
  1.1 7.5 %copy-start = (f32[2,131072]{1,0:T(2,128)S(1)}, f32[2,131072]{1,0:T(2,128)}, u32[]{:S(2)}) copy-start(f32[2,131072]{1,0:T(2,128)} %param.5) | copy-start | bytes 3145732
  1.1 9.3 %collective-permute-start = (f32[1,512,128]{2,1,0:T(8,128)S(1)}, f32[1,512,128]{2,1,0:T(8,128)S(1)}, u32[]{:S(2)}, u32[]{:S(2)}) collective-permute-start(f32[1,512,128]{2,1,0:T(8,128)S(1)} %get-tuple-element.48), channel_id=1, source_target_pairs={{0,2},{1,3},{2,0},{3,1},{4,6},{5,7},{6,4},{7,5},{8,10},{9,11},{10,... | collective-permute-start | bytes 786440 | tf_op jit(solution)/shard_map/ppermute | solution.py:406
  9.1 10.4 %collective-permute-start.1 = (f32[2,512,128]{2,1,0:T(8,128)S(1)}, f32[2,512,128]{2,1,0:T(8,128)S(1)}, u32[]{:S(2)}, u32[]{:S(2)}) collective-permute-start(f32[2,512,128]{2,1,0:T(8,128)S(1)} %shard_map.56.refs_2_), channel_id=1, source_target_pairs={{0,1},{1,0},{2,3},{3,2},{4,5},{5,4},{6,7},{7,6},{8,9},{9,8},{10,11... | collective-permute-start | bytes 1572872 | tf_op jit(solution)/shard_map/ppermute | solution.py:406
  9.2 8.7 %collective-permute-start.4 = (f32[1,512,128]{2,1,0:T(8,128)S(1)}, f32[1,512,128]{2,1,0:T(8,128)S(1)}, u32[]{:S(2)}, u32[]{:S(2)}) collective-permute-start(f32[1,512,128]{2,1,0:T(8,128)S(1)} %get-tuple-element.47), channel_id=1, source_target_pairs={{0,2},{1,3},{2,0},{3,1},{4,6},{5,7},{6,4},{7,5},{8,10},{9,11},{10,... | collective-permute-start | bytes 786440 | tf_op jit(solution)/shard_map/ppermute | solution.py:406
  10.8 8.7 %collective-permute-start.2 = (f32[1,512,128]{2,1,0:T(8,128)S(1)}, f32[1,512,128]{2,1,0:T(8,128)S(1)}, u32[]{:S(2)}, u32[]{:S(2)}) collective-permute-start(f32[1,512,128]{2,1,0:T(8,128)S(1)} %shard_map.58.refs_4_), channel_id=1, source_target_pairs={{0,1},{1,0},{2,3},{3,2},{4,5},{5,4},{6,7},{7,6},{8,9},{9,8},{10,11... | collective-permute-start | bytes 786440 | tf_op jit(solution)/shard_map/ppermute | solution.py:406
  18.3 2.4 %collective-permute-start.5 = (f32[1,512,128]{2,1,0:T(8,128)S(1)}, f32[1,512,128]{2,1,0:T(8,128)S(1)}, u32[]{:S(2)}, u32[]{:S(2)}) collective-permute-start(f32[1,512,128]{2,1,0:T(8,128)S(1)} %shard_map.61.refs_4_), channel_id=1, source_target_pairs={{0,1},{1,0},{2,3},{3,2},{4,5},{5,4},{6,7},{7,6},{8,9},{9,8},{10,11... | collective-permute-start | bytes 786440 | tf_op jit(solution)/shard_map/ppermute | solution.py:406
  20.3 9.2 %collective-permute-start.3 = (f32[1,512,128]{2,1,0:T(8,128)S(1)}, f32[1,512,128]{2,1,0:T(8,128)S(1)}, u32[]{:S(2)}, u32[]{:S(2)}) collective-permute-start(f32[1,512,128]{2,1,0:T(8,128)S(1)} %shard_map.60), channel_id=1, source_target_pairs={{0,2},{1,3},{2,0},{3,1},{4,6},{5,7},{6,4},{7,5},{8,10},{9,11},{10,... | collective-permute-start | bytes 786440 | tf_op jit(solution)/shard_map/ppermute | solution.py:406
  21.4 13.3 %collective-permute-start.6 = (f32[1,512,128]{2,1,0:T(8,128)S(1)}, f32[1,512,128]{2,1,0:T(8,128)S(1)}, u32[]{:S(2)}, u32[]{:S(2)}) collective-permute-start(f32[1,512,128]{2,1,0:T(8,128)S(1)} %shard_map.63), channel_id=1, source_target_pairs={{0,2},{1,3},{2,0},{3,1},{4,6},{5,7},{6,4},{7,5},{8,10},{9,11},{10,... | collective-permute-start | bytes 786440 | tf_op jit(solution)/shard_map/ppermute | solution.py:406

commit v5 on v4

--- a/solution.py
+++ b/solution.py
@@ -194,7 +194,7 @@
     return ref[at, pl.ds(0, rows, stride=2), :], ref[at, pl.ds(1, rows, stride=2), :]
 
 
-def front_kernel(order, starts, pair, unit, w0_ref, w1_ref, units, flags, coef, *scratch):
+def front_kernel(order, starts, pair, unit, w0_ref, w1_ref, re, im, units, flags, coef, *scratch):
     order_s, starts_s, pair_s, u, m_re, m_im, small_sems, sems, late_sems = scratch
     ngates, later, gdim = unit.shape[0], units.shape[0], unit.shape[-1]
     count, half = ngates - later, gdim // 2
@@ -239,6 +239,8 @@
             r += v_re * x_re - v_im * x_im
             i += v_re * x_im + v_im * x_re
         w1_ref[0, k], w1_ref[1, k] = split(embed(r, i))
+    late(0).wait()
+    begin(units[0, 0], units[0, 1], starts_s[count], 0, (re, im))
     bits = starts_s[count]
     for k in range(1, later):
         bits += starts_s[count + k] * 2**k
@@ -249,7 +251,8 @@
                 coef[i, b, p] = jnp.full(coef.shape[3:], v, F32)
     for k in range(later):
         fetch(order_s[count + k]).wait()
-        late(k).wait()
+        if k:
+            late(k).wait()
 
 
 def chosen(units, flags):
@@ -261,8 +264,12 @@
     return gate
 
 
-def half_kernel(units, flags, re, im):
-    compose(units.shape[0] // 2, 0, chosen(units, flags), (re, im))
+def half_kernel(units, flags, re1, im1, re, im):
+    gate = chosen(units, flags)
+    source = (re1, im1)
+    for k in range(1, units.shape[0] // 2):
+        apply(*gate(k), source, (re, im))
+        source = (re, im)
 
 
 def third_kernel(units, flags, re, im, w_ref, m_re, m_im):
@@ -419,11 +426,13 @@
     ngates = unitaries.shape[0]
     tile = (8, lanes)
     dma = pltpu.SemaphoreType.DMA
-    w0, w1, units, flags, coef = call(
+    w0, w1, re1, im1, units, flags, coef = call(
         front_kernel,
         [
             bf16((2, 3, dim, dim)),
             bf16((2, 2, half, rows)),
+            m,
+            m,
             f32((count, *unitaries.shape[1:])),
             jax.ShapeDtypeStruct(tile, jnp.int32),
             f32((2, 2, 2, *tile)),
@@ -438,7 +447,7 @@
     (kept,) = call(kept_kernel, [both], [w0, view], [VM] * 2, flops=2 * enter_flops)
     kept_other = other(kept, 1)
     units, kept = tie((units, kept))
-    re2, im2 = call(half_kernel, [m, m], [units, flags], [VM] * 2, flops=count * step // 2)
+    re2, im2 = call(half_kernel, [m, m], [units, flags, re1, im1], [VM] * 4, flops=step)
     came[0], re2 = tie((came[0], re2))
     (mine,) = call(came_kernel, [block], [w0, came[0]], [VM] * 2, flops=enter_flops)
     re2, mine = tie((re2, mine))

time: 35.7 us -> 36 us (level)
  waiting for transfers between devices: 16 us -> 16.4 us
where the time goes in v5:
time: 36 us; the launch traced here: 35.8 us
  waiting for transfers between devices  16.4 us (46%)
  Pallas kernels  12.5 us (35%)
  starting transfers between devices  5.72 us (16%)
  local copies, waits for them, and re-layouts  1.07 us (3%)
    ppermute x7, waiting for transfers between devices, other(): return lax.ppermute(v, 'qa', [(i, i ^ bit) for i in range(devices)])  16.4 us
    pallas_call x10, Pallas kernels, call(): pl.pallas_call(body, out_shape=outs, in_specs=specs, out_specs=[VM] * len...  10.8 us
    ppermute x7, starting transfers between devices, other(): return lax.ppermute(v, 'qa', [(i, i ^ bit) for i in range(devices)])  5.72 us
    pallas_call x2, Pallas kernels, finish(): pl.pallas_call(partial(last_kernel, chunk), out_shape=shape, in_specs=[VM...  1.68 us
    dynamic_slice x1, local copies, waits for them, and re-layouts, block_of(): return lax.dynamic_slice_in_dim(v, (1 - h1) * 2 + c, 1, axis=0)  1.06 us
  transfers between devices with their start and end apart: 7, of which 4 were waited for; matrix products, arithmetic and copies ran while one was open for 0% of the time, Pallas kernels for 33%

profile of v5, /device:TPU:0, one launch (start us, length us, event | category | flops | bytes accessed | tf_op | source)
XLA Modules:
  0.0 35.8 jit_solution(9300566988412851563)
XLA Ops:
  0.0 1.1 %constant_dynamic-slice_fusion = (f32[1,512,128]{2,1,0:T(8,128)S(1)}, f32[1,512,128]{2,1,0:T(8,128)S(1)}) fusion(f32[4,512,128]{2,1,0:T(8,128)} %bitcast.10, s32[]{:T(128)S(6)} %select_n.7, s32[]{:T(128)S(6)} %select_n.6), kind=kLoop, calls=%fused_computation | loop fusion | bytes 1048584 | tf_op jit(solution)/shard_map/dynamic_slice | solution.py:416
  1.1 0.0 copy-start
  1.1 3.0 %collective-permute-start = (f32[1,512,128]{2,1,0:T(8,128)S(1)}, f32[1,512,128]{2,1,0:T(8,128)S(1)}, u32[]{:S(2)}, u32[]{:S(2)}) collective-permute-start(f32[1,512,128]{2,1,0:T(8,128)S(1)} %get-tuple-element.52), channel_id=1, source_target_pairs={{0,2},{1,3},{2,0},{3,1},{4,6},{5,7},{6,4},{7,5},{8,10},{9,11},{10,... | collective-permute-start | bytes 786440 | tf_op jit(solution)/shard_map/ppermute | solution.py:413
  4.1 4.8 %shard_map.55 = (bf16[2,3,256,256]{3,2,1,0:T(8,128)(2,1)S(1)}, bf16[2,2,128,512]{3,2,1,0:T(8,128)(2,1)S(1)}, f32[2,256,128]{2,1,0:T(8,128)S(1)}, f32[2,256,128]{...) custom-call(s32[12]{0:T(128)} %order.1, s32[12]{0:T(128)} %starts.1, ...), custom_call_target="tpu_custom_call" | custom-call | flops 1610612736 | bytes 3969184 | tf_op jit(solution)/shard_map/pallas_call | solution.py:375
  8.9 0.0 copy-done
  8.9 0.5 %shard_map.56.refs_2_ = f32[2,512,128]{2,1,0:T(8,128)S(1)} custom-call(bf16[2,3,256,256]{3,2,1,0:T(8,128)(2,1)S(1)} %get-tuple-element.30.w_ref, f32[4,512,128]{2,1,0:T(8,128)S(1)} %bitcast.11), custom_call_target="tpu_custom_call" | custom-call | flops 402653184 | bytes 2359296 | tf_op jit(solution)/shard_map/pallas_call | solution.py:375
  9.4 0.1 collective-permute-start.1
  9.5 0.2 collective-permute-start.4
  9.6 0.6 %shard_map.57 = (f32[2,256,128]{2,1,0:T(8,128)S(1)}, f32[2,256,128]{2,1,0:T(8,128)S(1)}) custom-call(f32[4,2,128,128]{3,2,1,0:T(8,128)S(1)} %get-tuple-element.31.units, s32[8,128]{1,0:T(8,128)S(1)} %get-tuple-element.32.flags, f32[2,256,128]{2,1,0:T(8,128)S(1)} %get-tuple-element.33.re1, f32[2,256,128]{2,1,0:T(8,128)S(1)} %get-tuple-element.34.im1), custom_call_target="tpu_custom_call" | custom-call | flops 201326592 | bytes 1576960 | tf_op jit(solution)/shard_map/pallas_call | solution.py:375
  10.2 0.2 collective-permute-done.raw
  10.4 0.4 %shard_map.58.refs_4_ = f32[1,512,128]{2,1,0:T(8,128)S(1)} custom-call(bf16[2,3,256,256]{3,2,1,0:T(8,128)(2,1)S(1)} %get-tuple-element.30.w_ref, f32[1,512,128]{2,1,0:T(8,128)S(1)} %collective-permute-done.raw), custom_call_target="tpu_custom_call" | custom-call | flops 201326592 | bytes 1310720 | tf_op jit(solution)/shard_map/pallas_call | solution.py:375
  10.8 0.2 collective-permute-start.2
  11.0 7.2 %collective-permute-done.4.raw = f32[1,512,128]{2,1,0:T(8,128)S(1)} collective-permute-done((f32[1,512,128]{2,1,0:T(8,128)S(1)}, f32[1,512,128]{2,1,0:T(8,128)S(1)}, u32[]{:S(2)}, u32[]{:S(2)}) %collective-permute-start.4) | collective-permute-done | bytes 262176 | tf_op jit(solution)/shard_map/ppermute | solution.py:413
  18.2 0.4 %shard_map.61.refs_4_ = f32[1,512,128]{2,1,0:T(8,128)S(1)} custom-call(bf16[2,3,256,256]{3,2,1,0:T(8,128)(2,1)S(1)} %get-tuple-element.30.w_ref, f32[1,512,128]{2,1,0:T(8,128)S(1)} %collective-permute-done.4.raw), custom_call_target="tpu_custom_call" | custom-call | flops 201326592 | bytes 1310720 | tf_op jit(solution)/shard_map/pallas_call | solution.py:375
  18.6 0.1 collective-permute-start.5
  18.7 1.1 %shard_map.59.refs_1_ = bf16[2,3,256,256]{3,2,1,0:T(8,128)(2,1)S(1)} custom-call(f32[4,2,128,128]{3,2,1,0:T(8,128)S(1)} %get-tuple-element.31.units, s32[8,128]{1,0:T(8,128)S(1)} %get-tuple-element.32.flags, f32[2,256,128]{2,1,0:T(8,128)S(1)} %get-tuple-element.38.re, f32[2,256,128]{2,1,0:T(8,128)S(1)} %get-tuple-element.39.im), custom_call_target="tpu_custom_call" | custom-call | flops 402653184 | bytes 1839104 | tf_op jit(solution)/shard_map/pallas_call | solution.py:375
  19.8 0.0 collective-permute-done.2.refs_5_
  19.8 0.0 collective-permute-done.1.refs_3_
  19.8 0.8 %shard_map.60 = f32[1,512,128]{2,1,0:T(8,128)S(1)} custom-call(bf16[2,2,128,512]{3,2,1,0:T(8,128)(2,1)S(1)} %get-tuple-element.47.refs_0_, bf16[2,3,256,256]{3,2,1,0:T(8,128)(2,1)S(1)} %shard_map.59.refs_1_, f32[2,512,128]{2,1,0:T(8,128)S(1)} %shard_map.56.refs_2_, f32[2,512,128]{2,1,0:T(8,128)S(1)} %collective-permute-done.1.refs_3_, ...), custom_call_target="tpu_custom_call" | custom-call | flops 402653184 | bytes 3145728 | tf_op jit(solution)/shard_map/pallas_call | solution.py:375
  20.6 0.4 collective-permute-start.3
  21.0 0.0 collective-permute-done.5.refs_5_
  21.0 0.8 %shard_map.63 = f32[1,512,128]{2,1,0:T(8,128)S(1)} custom-call(bf16[2,2,128,512]{3,2,1,0:T(8,128)(2,1)S(1)} %get-tuple-element.47.refs_0_, bf16[2,3,256,256]{3,2,1,0:T(8,128)(2,1)S(1)} %shard_map.59.refs_1_, f32[2,512,128]{2,1,0:T(8,128)S(1)} %shard_map.56.refs_2_, f32[2,512,128]{2,1,0:T(8,128)S(1)} %collective-permute-done.1.refs_3_, ...), custom_call_target="tpu_custom_call" | custom-call | flops 402653184 | bytes 3145728 | tf_op jit(solution)/shard_map/pallas_call | solution.py:375
  21.7 1.8 %collective-permute-start.6 = (f32[1,512,128]{2,1,0:T(8,128)S(1)}, f32[1,512,128]{2,1,0:T(8,128)S(1)}, u32[]{:S(2)}, u32[]{:S(2)}) collective-permute-start(f32[1,512,128]{2,1,0:T(8,128)S(1)} %shard_map.63), channel_id=1, source_target_pairs={{0,2},{1,3},{2,0},{3,1},{4,6},{5,7},{6,4},{7,5},{8,10},{9,11},{10,... | collective-permute-start | bytes 786440 | tf_op jit(solution)/shard_map/ppermute | solution.py:413
  23.5 0.8 %shard_map.62 = (f32[1,512,128]{2,1,0:T(8,128)S(1)}, f32[1,512,128]{2,1,0:T(8,128)S(1)}) custom-call(f32[2,2,2,8,128]{4,3,2,1,0:T(8,128)S(1)} %get-tuple-element.42.coef, bf16[2,2,128,512]{3,2,1,0:T(8,128)(2,1)S(1)} %get-tuple-element.47.refs_0_, bf16[2,3,256,256]{3,2,1,0:T(8,128)(2,1)S(1)} %shard_map.59.refs_1_, f32[2,512,128]{2,1,0:T(8,128)S(1)} %shard_map.56.refs_2_, ...), custom_call_target="tpu_custom_call" | custom-call | flops 402653184 | bytes 3440640 | tf_op jit(solution)/shard_map/pallas_call | solution.py:375
  24.3 0.8 %shard_map.64 = (f32[1,512,128]{2,1,0:T(8,128)S(1)}, f32[1,512,128]{2,1,0:T(8,128)S(1)}) custom-call(f32[2,2,2,8,128]{4,3,2,1,0:T(8,128)S(1)} %get-tuple-element.42.coef, bf16[2,2,128,512]{3,2,1,0:T(8,128)(2,1)S(1)} %get-tuple-element.47.refs_0_, bf16[2,3,256,256]{3,2,1,0:T(8,128)(2,1)S(1)} %shard_map.59.refs_1_, f32[2,512,128]{2,1,0:T(8,128)S(1)} %shard_map.56.refs_2_, ...), custom_call_target="tpu_custom_call" | custom-call | flops 402653184 | bytes 3440640 | tf_op jit(solution)/shard_map/pallas_call | solution.py:375
  25.1 4.7 %collective-permute-done.3.back = f32[1,512,128]{2,1,0:T(8,128)S(1)} collective-permute-done((f32[1,512,128]{2,1,0:T(8,128)S(1)}, f32[1,512,128]{2,1,0:T(8,128)S(1)}, u32[]{:S(2)}, u32[]{:S(2)}) %collective-permute-start.3) | collective-permute-done | bytes 262176 | tf_op jit(solution)/shard_map/ppermute | solution.py:413
  29.8 0.8 %shard_map.65.refs_0_ = f32[2,2,512,128]{3,2,1,0:T(8,128)} custom-call(f32[1,512,128]{2,1,0:T(8,128)S(1)} %get-tuple-element.48.part0, f32[1,512,128]{2,1,0:T(8,128)S(1)} %get-tuple-element.49.part1, f32[1,512,128]{2,1,0:T(8,128)S(1)} %collective-permute-done.3.back, f32[2,2,2,8,128]{4,3,2,1,0:T(8,128)S(1)} %get-tuple-element.42.coef), custom_call_target="tpu_custom_call" | custom-call | bytes 1835008 | tf_op jit(solution)/shard_map/pallas_call | solution.py:389
  30.7 4.3 %collective-permute-done.6.back = f32[1,512,128]{2,1,0:T(8,128)S(1)} collective-permute-done((f32[1,512,128]{2,1,0:T(8,128)S(1)}, f32[1,512,128]{2,1,0:T(8,128)S(1)}, u32[]{:S(2)}, u32[]{:S(2)}) %collective-permute-start.6) | collective-permute-done | bytes 262176 | tf_op jit(solution)/shard_map/ppermute | solution.py:413
  35.0 0.8 %shard_map.66 = f32[2,2,512,128]{3,2,1,0:T(8,128)} custom-call(f32[1,512,128]{2,1,0:T(8,128)S(1)} %get-tuple-element.45.part0, f32[1,512,128]{2,1,0:T(8,128)S(1)} %get-tuple-element.46.part1, f32[1,512,128]{2,1,0:T(8,128)S(1)} %collective-permute-done.6.back, f32[2,2,2,8,128]{4,3,2,1,0:T(8,128)S(1)} %get-tuple-element.42.coef, ...), custom_call_target="tpu_custom_call", output_to_operand_aliasing={{}: (4, {})} | custom-call | bytes 1835008 | tf_op jit(solution)/shard_map/pallas_call | solution.py:389
Async XLA Ops:
  1.1 7.8 %copy-start = (f32[2,131072]{1,0:T(2,128)S(1)}, f32[2,131072]{1,0:T(2,128)}, u32[]{:S(2)}) copy-start(f32[2,131072]{1,0:T(2,128)} %param.5) | copy-start | bytes 3145732
  1.1 9.3 %collective-permute-start = (f32[1,512,128]{2,1,0:T(8,128)S(1)}, f32[1,512,128]{2,1,0:T(8,128)S(1)}, u32[]{:S(2)}, u32[]{:S(2)}) collective-permute-start(f32[1,512,128]{2,1,0:T(8,128)S(1)} %get-tuple-element.52), channel_id=1, source_target_pairs={{0,2},{1,3},{2,0},{3,1},{4,6},{5,7},{6,4},{7,5},{8,10},{9,11},{10,... | collective-permute-start | bytes 786440 | tf_op jit(solution)/shard_map/ppermute | solution.py:413
  9.4 10.4 %collective-permute-start.1 = (f32[2,512,128]{2,1,0:T(8,128)S(1)}, f32[2,512,128]{2,1,0:T(8,128)S(1)}, u32[]{:S(2)}, u32[]{:S(2)}) collective-permute-start(f32[2,512,128]{2,1,0:T(8,128)S(1)} %shard_map.56.refs_2_), channel_id=1, source_target_pairs={{0,1},{1,0},{2,3},{3,2},{4,5},{5,4},{6,7},{7,6},{8,9},{9,8},{10,11... | collective-permute-start | bytes 1572872 | tf_op jit(solution)/shard_map/ppermute | solution.py:413
  9.5 8.7 %collective-permute-start.4 = (f32[1,512,128]{2,1,0:T(8,128)S(1)}, f32[1,512,128]{2,1,0:T(8,128)S(1)}, u32[]{:S(2)}, u32[]{:S(2)}) collective-permute-start(f32[1,512,128]{2,1,0:T(8,128)S(1)} %get-tuple-element.51), channel_id=1, source_target_pairs={{0,2},{1,3},{2,0},{3,1},{4,6},{5,7},{6,4},{7,5},{8,10},{9,11},{10,... | collective-permute-start | bytes 786440 | tf_op jit(solution)/shard_map/ppermute | solution.py:413
  10.8 9.0 %collective-permute-start.2 = (f32[1,512,128]{2,1,0:T(8,128)S(1)}, f32[1,512,128]{2,1,0:T(8,128)S(1)}, u32[]{:S(2)}, u32[]{:S(2)}) collective-permute-start(f32[1,512,128]{2,1,0:T(8,128)S(1)} %shard_map.58.refs_4_), channel_id=1, source_target_pairs={{0,1},{1,0},{2,3},{3,2},{4,5},{5,4},{6,7},{7,6},{8,9},{9,8},{10,11... | collective-permute-start | bytes 786440 | tf_op jit(solution)/shard_map/ppermute | solution.py:413
  18.6 2.4 %collective-permute-start.5 = (f32[1,512,128]{2,1,0:T(8,128)S(1)}, f32[1,512,128]{2,1,0:T(8,128)S(1)}, u32[]{:S(2)}, u32[]{:S(2)}) collective-permute-start(f32[1,512,128]{2,1,0:T(8,128)S(1)} %shard_map.61.refs_4_), channel_id=1, source_target_pairs={{0,1},{1,0},{2,3},{3,2},{4,5},{5,4},{6,7},{7,6},{8,9},{9,8},{10,11... | collective-permute-start | bytes 786440 | tf_op jit(solution)/shard_map/ppermute | solution.py:413
  20.6 9.2 %collective-permute-start.3 = (f32[1,512,128]{2,1,0:T(8,128)S(1)}, f32[1,512,128]{2,1,0:T(8,128)S(1)}, u32[]{:S(2)}, u32[]{:S(2)}) collective-permute-start(f32[1,512,128]{2,1,0:T(8,128)S(1)} %shard_map.60), channel_id=1, source_target_pairs={{0,2},{1,3},{2,0},{3,1},{4,6},{5,7},{6,4},{7,5},{8,10},{9,11},{10,... | collective-permute-start | bytes 786440 | tf_op jit(solution)/shard_map/ppermute | solution.py:413
  21.7 13.3 %collective-permute-start.6 = (f32[1,512,128]{2,1,0:T(8,128)S(1)}, f32[1,512,128]{2,1,0:T(8,128)S(1)}, u32[]{:S(2)}, u32[]{:S(2)}) collective-permute-start(f32[1,512,128]{2,1,0:T(8,128)S(1)} %shard_map.63), channel_id=1, source_target_pairs={{0,2},{1,3},{2,0},{3,1},{4,6},{5,7},{6,4},{7,5},{8,10},{9,11},{10,... | collective-permute-start | bytes 786440 | tf_op jit(solution)/shard_map/ppermute | solution.py:413
